TPU v7x, 128 devices: a whole 4x4x4 slice. The times are simulated.
128 devices in a mesh: row: 16 (over x, z), col: 8 (over y, core).
Axes of the slice: x: 4, y: 4, z: 4, core: 2. Of those that a mesh axis runs over, the one named last changes fastest.
Arguments:
- hole_panel: bfloat16 [8192, 98304], P('row', 'col'), may hold values from -0.0546875 to 0.0546875
- amplitudes: bfloat16 [768, 98304], P(('row', 'col')), may hold values from -6 to 6
- row_sizes: int32 [8], replicated, may hold values from 1 to 2048, 8192 in all
- col_sizes: int32 [8], replicated, may hold values from 1 to 24576, 98304 in all
- pair_order: int32 [768], replicated, may hold values from 0 to 767, each once
Outputs:
- cycle_term: float32 [8192, 768], P('row', 'col')
Inputs may be any that keep to these rules, and one draw needn't show every extreme that they name: `row_sizes`: the rows of irrep g follow those of the irreps below g; the sizes sum to 8192, the largest is 2048. `col_sizes`: the indices of irrep g follow those of the irreps below g; the sizes sum to 98304, the largest is 24576. `pair_order`: each pair appears once.
All inputs are finite; a program needn't handle non-finite values.
Results may differ from a plain program's by a relative error of at most 0.0003.
Values may be sent and summed in bfloat16 or wider, within the bound.
No kernel may reach another device: no remote copies, remote signals or barrier semaphores. Data moves between devices by JAX's collectives and lax.ppermute only.
A program may use at most 192 MiB of HBM per device.

v0:
```python
import jax
import jax.numpy as jnp
from jax import lax
from jax.sharding import PartitionSpec as P


def irrep_labels(sizes, count, offset):
    position = offset + lax.iota(jnp.int32, count)
    bounds = jnp.cumsum(sizes)
    return jnp.sum((position[:, None] >= bounds[None, :]).astype(jnp.int32), axis=1)


def contract(masked, piece):
    numbers = (((1,), (1,)), ((), ()))
    return lax.dot_general(masked, piece, numbers, preferred_element_type=jnp.float32)


def on_device(hole_panel, amplitudes, row_sizes, col_sizes, pair_order):
    row_count, col_count = hole_panel.shape
    row_devices = lax.axis_size("row")
    col_devices = lax.axis_size("col")
    per_device = amplitudes.shape[0]
    pair_total = per_device * row_devices * col_devices
    row_irrep = irrep_labels(row_sizes, row_count, lax.axis_index("row") * row_count)
    col_irrep = irrep_labels(col_sizes, col_count, lax.axis_index("col") * col_count)
    masked = jnp.where(
        row_irrep[:, None] == col_irrep[None, :], hole_panel, jnp.zeros((), hole_panel.dtype)
    )
    split_rows = lax.all_to_all(amplitudes, "col", split_axis=1, concat_axis=0, tiled=True)
    stored = contract(masked, lax.all_gather(split_rows, "row", axis=0, tiled=True))
    logical = jnp.zeros((row_count, pair_total), jnp.float32).at[:, pair_order].set(stored)
    return lax.psum_scatter(logical, "col", scatter_dimension=1, tiled=True)


def solution(mesh):
    in_specs = (P("row", "col"), P(("row", "col"), None), P(), P(), P())
    out_specs = P("row", "col")
    return jax.shard_map(
        on_device, mesh=mesh, in_specs=in_specs, out_specs=out_specs, check_vma=False
    )
```

profile of v0, /device:TPU:6, one launch (start us, length us, event | category | flops | bytes accessed | tf_op | source)
XLA Modules:
  0.0 220.9 jit_solution(13136093127057807586)
XLA Ops:
  6.5 0.0 all-gather.2.cloned.1.call-start
  6.5 26.3 %all_to_all.19 = bf16[6,8,12288]{2,0,1:T(8,128)(2,1)S(1)} all-to-all(bf16[6,8,12288]{2,0,1:T(8,128)(2,1)} %bitcast.10), channel_id=1, replica_groups=mesh['row'=16,'col'=8] {'col'}, dimensions={1} | all-to-all | bytes 2359296 | tf_op jit(solution)/shard_map/all_to_all | solution.py:29
  32.8 0.0 copy-start.1
  32.8 0.0 copy-start.2
  32.8 0.0 copy-start
  32.8 1.3 all_to_all.17
  34.1 0.0 all-gather.2.cloned.1.call-update
  34.1 0.0 reduce-scatter.2.cloned.1.call-start
  34.2 0.0 copy-done.1
  34.2 0.2 reduce-window.17
  34.4 0.0 copy-done.2
  34.4 0.2 reduce-window.16
  34.6 0.1 convert_reduce_fusion.1
  34.7 0.2 convert_reduce_fusion
  34.9 0.0 copy-done
  34.9 121.8 %all-gather.2.cloned.1.call-done = bf16[768,12288]{1,0:T(8,128)(2,1)} async-done(((bf16[48,12288]{1,0:T(8,128)(2,1)}), bf16[768,12288]{1,0:T(8,128)(2,1)}) %all-gather.2.cloned.1.call-update) | async-done | bytes 18874384 | tf_op jit(solution)/shard_map/all_gather | solution.py:30
  156.7 17.6 %fusion.4 = f32[768,512]{0,1:T(8,128)S(1)} fusion(bf16[768,12288]{1,0:T(8,128)(2,1)} %all-gather.2.cloned.1.call-done, bf16[512,12288]{1,0:T(8,128)(2,1)} %param.5, s32[12288]{0:T(1024)S(1)} %convert_reduce_fusion, s32[512]{0:T(512)S(1)} %convert_reduce_fusion.1), kind=kOutput, calls=%fused_computation.6 | convolution fusion | flops 9676259328 | bytes 33081344 | tf_op jit(solution)/shard_map/dot_general | solution.py:15
  174.4 0.5 copy.10
  174.8 6.7 %scatter_custom_fusion = f32[512,768]{0,1:T(8,128)} fusion(s32[768]{0:T(1024)S(1)} %compare_select_fusion.4, f32[768,512]{1,0:T(8,128)S(1)} %copy.10, f32[]{:T(128)} %constant.9.clone.1), kind=kCustom, calls=%fused_computation.7 | custom fusion | bytes 1572868 | tf_op jit(solution)/shard_map/scatter | solution.py:31
  181.6 0.0 reduce-scatter.2.cloned.1.call-update
  181.6 32.5 %reduce-scatter.2.cloned.1.call-done = f32[512,96]{0,1:T(8,128)} async-done(((f32[512,768]{0,1:T(8,128)}), f32[512,96]{0,1:T(8,128)}) %reduce-scatter.2.cloned.1.call-update) | async-done | bytes 196624 | tf_op jit(solution)/shard_map/reduce_scatter | solution.py:32
  (3 shorter events, 0.0 us)
Async XLA Ops:
  6.5 150.2 %all-gather.2.cloned.1.call-start = ((), (), s32[]{:S(2)}) async-start(), calls=%async_computation.2 | async-start | bytes 20054016 | tf_op jit(solution)/shard_map/all_gather | solution.py:30
  32.8 1.4 copy-start.1
  32.8 1.6 copy-start.2
  32.8 2.1 copy-start
  34.1 179.9 %reduce-scatter.2.cloned.1.call-start = ((), (), s32[]{:S(2)}) async-start(), calls=%async_computation.3 | async-start | bytes 1769472 | tf_op jit(solution)/shard_map/reduce_scatter | solution.py:32
Sparse Core Ops, SparseCore 0:
  34.3 122.4 all-gather.1
  181.7 32.3 reduce-scatter.1
where the time goes:
time: 221 us
  waiting for transfers between devices  154 us (70%)
  blocking collectives  26.3 us (12%)
  matrix products  17.6 us (8%)
  between operations  13.5 us (6%)
  local copies, waits for them, and re-layouts  8.5 us (4%)
    all_gather x1, waiting for transfers between devices, on_device(): lax.all_gather(split_rows, 'row', axis=0, tiled=True)  122 us
    reduce_scatter x1, waiting for transfers between devices, on_device(): return lax.psum_scatter(logical, 'col', scatter_dimension=1, tiled=True)  32.5 us
    all_to_all x1, blocking collectives, on_device(): lax.all_to_all(amplitudes, 'col', split_axis=1, concat_axis=0, tiled=True)  26.3 us
    dot_general x1, matrix products, contract(): lax.dot_general(masked, piece, numbers, preferred_element_type=jnp.float32)  17.6 us
    scatter x1, local copies, waits for them, and re-layouts, on_device(): jnp.zeros((row_count, pair_total), jnp.float32).at[:, pair_order]  6.72 us
  transfers between devices with their start and end apart: 2, of which 2 were waited for; matrix products, arithmetic and copies ran while one was open for 0% of the time, Pallas kernels for 0%

commit v1 on v0

v1 whole, which is shorter than its diff:
```python
import functools

import jax
import jax.numpy as jnp
from jax import lax
from jax.experimental import pallas as pl
from jax.experimental.pallas import tpu as pltpu
from jax.sharding import PartitionSpec as P

SIDE = 4
CORES = 2
K_BLOCKS = 8


def irrep_labels(sizes, count, offset):
    position = offset + lax.iota(jnp.int32, count)
    bounds = jnp.cumsum(sizes)
    return jnp.sum((position[:, None] >= bounds[None, :]).astype(jnp.int32), axis=1)


def device_pairs(move):
    pairs = []
    for x in range(SIDE):
        for z in range(SIDE):
            for y in range(SIDE):
                for core in range(CORES):
                    to_x, to_z, to_y, to_core = move(x, z, y, core)
                    to = (to_x % SIDE) * SIDE + to_z % SIDE
                    pairs.append((
                        ((x * SIDE + z) * SIDE + y) * CORES + core,
                        (to * SIDE + to_y % SIDE) * CORES + to_core % CORES,
                    ))
    return pairs


def along_first(value, step):
    def move(x, z, y, core):
        return (x + step, z, y, core) if core == 0 else (x, z + step, y, core)
    return lax.ppermute(value, ("row", "col"), device_pairs(move))


def along_second(value, step):
    def move(x, z, y, core):
        return (x, z + step, y, core) if core == 0 else (x + step, z, y, core)
    return lax.ppermute(value, ("row", "col"), device_pairs(move))


def along_y(value, step):
    return lax.ppermute(
        value, ("row", "col"), device_pairs(lambda x, z, y, core: (x, z, y + step, core))
    )


def to_other_core(value):
    return lax.ppermute(
        value, ("row", "col"), device_pairs(lambda x, z, y, core: (x, z, y, core + 1))
    )


def product(piece, panel):
    numbers = (((1,), (1,)), ((), ()))
    return lax.dot_general(piece, panel, numbers, preferred_element_type=jnp.float32)


def place_rows(place_ref, total_ref, out_ref, rows):
    def body(row, carry):
        out_ref[pl.ds(place_ref[row], 1), :] = total_ref[pl.ds(row, 1), :]
        return carry
    lax.fori_loop(0, rows, body, 0, unroll=8)


def early_kernel(place_ref, panel_ref, *refs):
    *piece_refs, out_ref, total_ref = refs
    step = pl.program_id(0)

    @pl.when(step == 0)
    def _():
        total_ref[...] = jnp.zeros_like(total_ref)

    panel = panel_ref[...]
    at = 0
    for piece_ref in piece_refs:
        rows = pl.ds(at, piece_ref.shape[0])
        total_ref[rows, :] += product(piece_ref[...], panel)
        at += piece_ref.shape[0]

    @pl.when(step == pl.num_programs(0) - 1)
    def _():
        place_rows(place_ref, total_ref, out_ref, at)


def early_product(place, panel, pieces):
    rows, depth = panel.shape
    block = depth // K_BLOCKS
    count = sum(piece.shape[0] for piece in pieces)
    pairs = count // (SIDE - 1) * SIDE
    return pl.pallas_call(
        early_kernel,
        out_shape=jax.ShapeDtypeStruct((pairs, rows), jnp.float32),
        grid_spec=pltpu.PrefetchScalarGridSpec(
            num_scalar_prefetch=1,
            grid=(K_BLOCKS,),
            in_specs=[pl.BlockSpec((value.shape[0], block), lambda k, place: (0, k))
                      for value in (panel, *pieces)],
            out_specs=pl.BlockSpec((pairs, rows), lambda k, place: (0, 0)),
            scratch_shapes=[pltpu.VMEM((count, rows), jnp.float32)],
        ),
        name="early_product",
    )(place, panel, *pieces)


def late_kernel(place_ref, panel_ref, low_ref, high_ref, left_ref, right_ref, early_ref,
                mine_ref, theirs_ref, total_ref, all_ref):
    step = pl.program_id(0)
    steps = pl.num_programs(0)
    panel = panel_ref[...]
    low_rows, high_rows = low_ref.shape[0], high_ref.shape[0]
    far_rows = left_ref.shape[0]

    @pl.when(step == 0)
    def _():
        total_ref[...] = jnp.zeros_like(total_ref)
        all_ref[...] = early_ref[...]

    total_ref[pl.ds(0, low_rows), :] += product(low_ref[...], panel)
    total_ref[pl.ds(low_rows, high_rows), :] += product(high_ref[...], panel)
    far = pl.ds(low_rows + high_rows, far_rows)

    @pl.when(step < steps // 2)
    def _():
        total_ref[far, :] += product(left_ref[...], panel)

    @pl.when(step >= steps // 2)
    def _():
        total_ref[far, :] += product(right_ref[...], panel)

    @pl.when(step == steps - 1)
    def _():
        place_rows(place_ref, total_ref, all_ref, low_rows + high_rows + far_rows)
        half = mine_ref.shape[0]
        mine_ref[...] = all_ref[pl.ds(0, half), :]
        theirs_ref[...] = all_ref[pl.ds(half, half), :]


def late_product(place, panel, low, high, left, right, early):
    rows, depth = panel.shape
    block = depth // K_BLOCKS
    count = low.shape[0] + high.shape[0] + left.shape[0]
    pairs = early.shape[0]
    middle = K_BLOCKS // 2
    whole = lambda value: pl.BlockSpec((value.shape[0], block), lambda k, place: (0, k))
    fixed = lambda height: pl.BlockSpec((height, rows), lambda k, place: (0, 0))
    return pl.pallas_call(
        late_kernel,
        out_shape=[jax.ShapeDtypeStruct((pairs // 2, rows), jnp.float32)] * 2,
        grid_spec=pltpu.PrefetchScalarGridSpec(
            num_scalar_prefetch=1,
            grid=(K_BLOCKS,),
            in_specs=[
                whole(panel), whole(low), whole(high),
                pl.BlockSpec((left.shape[0], block),
                             lambda k, place: (0, jnp.minimum(k, middle - 1))),
                pl.BlockSpec((right.shape[0], block),
                             lambda k, place: (0, jnp.maximum(k - middle, 0))),
                fixed(pairs),
            ],
            out_specs=[fixed(pairs // 2)] * 2,
            scratch_shapes=[pltpu.VMEM((count, rows), jnp.float32),
                            pltpu.VMEM((pairs, rows), jnp.float32)],
        ),
        name="late_product",
    )(place, panel, low, high, left, right, early)


def on_device(hole_panel, amplitudes, row_sizes, col_sizes, pair_order):
    row_count, col_count = hole_panel.shape
    col_devices = lax.axis_size("col")
    per_device = amplitudes.shape[0]
    unit = per_device * col_devices
    row_at, col_at = lax.axis_index("row"), lax.axis_index("col")
    my_x, my_z = row_at // SIDE, row_at % SIDE
    my_y, my_core = col_at // CORES, col_at % CORES

    out_pairs = pair_order.shape[0] // col_devices
    owner = pair_order // out_pairs
    block = (owner // CORES - my_y) % SIDE + SIDE * ((owner - my_core) % CORES)
    goes_to = (block * out_pairs + pair_order % out_pairs).astype(jnp.int32)
    by_unit = goes_to.reshape(SIDE, SIDE, col_devices, per_device).transpose(0, 1, 3, 2)
    by_unit = by_unit.reshape(SIDE, SIDE, unit)
    by_unit = jnp.where(my_core == 0, by_unit, by_unit.transpose(1, 0, 2))
    my_first = jnp.where(my_core == 0, my_x, my_z)
    my_second = jnp.where(my_core == 0, my_z, my_x)

    def places(second_hop):
        firsts = (my_first - jnp.array([0, 1, 3, 2])) % SIDE
        return by_unit[firsts, (my_second - second_hop) % SIDE].reshape(-1)

    early_places = jnp.concatenate([places(0), places(1), places(3)])
    late_places = places(2)

    split = amplitudes.reshape(per_device, col_devices, col_count)
    own = lax.all_to_all(split, "col", split_axis=1, concat_axis=1, tiled=True)
    own = own.reshape(unit, col_count)

    row_irrep = irrep_labels(row_sizes, row_count, row_at * row_count)
    col_irrep = irrep_labels(col_sizes, col_count, col_at * col_count)
    masked = jnp.where(
        row_irrep[:, None] == col_irrep[None, :], hole_panel, jnp.zeros((), hole_panel.dtype)
    )

    half = col_count // 2
    cut = unit + unit // 2
    back, ahead = along_first(own, 1), along_first(own, -1)
    far = jnp.concatenate(
        [along_first(back[:, :half], 1), along_first(ahead[:, half:], -1)], axis=1
    )
    near = jnp.concatenate([own, back, ahead], axis=0)
    near_1, near_3 = along_second(near, 1), along_second(near, -1)
    far_1, far_3 = along_second(far, 1), along_second(far, -1)
    near_2_low, near_2_high = along_second(near_1[:cut], 1), along_second(near_3[cut:], -1)
    far_2_left, far_2_right = along_second(far_1[:, :half], 1), along_second(far_3[:, half:], -1)

    early = early_product(early_places, masked, (near, far, near_1, far_1, near_3, far_3))
    mine, theirs = late_product(
        late_places, masked, near_2_low, near_2_high, far_2_left, far_2_right, early
    )
    shares = mine + to_other_core(theirs)
    total = shares[:out_pairs]
    for hop in (1, 3, 2):
        total = total + along_y(shares[hop * out_pairs:(hop + 1) * out_pairs], hop)
    return total.T


def solution(mesh):
    in_specs = (P("row", "col"), P(("row", "col"), None), P(), P(), P())
    out_specs = P("row", "col")
    return jax.shard_map(
        on_device, mesh=mesh, in_specs=in_specs, out_specs=out_specs, check_vma=False
    )
```

time: 221 us -> 200 us (0.905)
  waiting for transfers between devices: 154 us -> 63.8 us
  Pallas kernels: 0 us -> 49.7 us
  starting transfers between devices: 0.04 us -> 18.9 us
  matrix products: 17.6 us -> 0 us
  other arithmetic: 0.65 us -> 17 us
  local copies, waits for them, and re-layouts: 8.5 us -> 23.9 us
  between operations: 13.5 us -> 0.13 us
    all_gather x1 -> x0, waiting for transfers between devices: 122 us -> none  [on_device(): lax.all_gather(split_rows, 'row', axis=0, tiled=True)]
    ppermute x0 -> x16, waiting for transfers between devices: none -> 63.8 us  [the longest x4 29.6 us: along_first(): return lax.ppermute(value, ('row', 'col'), device_pairs(move))]
    pallas_call x0 -> x2, Pallas kernels: none -> 49.7 us  [the longest x1 30.3 us: early_product(): pl.pallas_call(early_kernel, out_shape=jax.ShapeDtypeStruct((pairs, rows)...]
    reduce_scatter x1 -> x0, waiting for transfers between devices: 32.5 us -> none  [on_device(): return lax.psum_scatter(logical, 'col', scatter_dimension=1, tiled=True)]
    ppermute x0 -> x16, starting transfers between devices: none -> 18.9 us  [the longest x8 11.4 us: along_second(): return lax.ppermute(value, ('row', 'col'), device_pairs(move))]
    dot_general x1 -> x0, matrix products: 17.6 us -> none  [contract(): lax.dot_general(masked, piece, numbers, preferred_element_type=jnp.float32)]
    select_n x1 -> x2, other arithmetic: 0.01 us -> 11.6 us  [the longest x1 11.6 us: on_device(): jnp.where(row_irrep[:, None] == col_irrep[None, :], hole_panel, jnp.zeros...]
    slice x0 -> x7, local copies, waits for them, and re-layouts: none -> 10.3 us  [the longest x1 2.86 us: on_device(): near_1[:cut]]
  transfers between devices with their start and end apart: 2 -> 16, of which waited for: 2 -> 7; matrix products, arithmetic and copies ran while one was open for 0% -> 18% of each run, Pallas kernels for 0% -> 15%
where the time goes in v1:
time: 200 us
  waiting for transfers between devices  63.8 us (32%)
  Pallas kernels  49.7 us (25%)
  blocking collectives  26.3 us (13%)
  local copies, waits for them, and re-layouts  23.9 us (12%)
  starting transfers between devices  18.9 us (9%)
  other arithmetic  17 us (8%)
    pallas_call x1, Pallas kernels, early_product(): pl.pallas_call(early_kernel, out_shape=jax.ShapeDtypeStruct((pairs, rows)...  30.3 us
    ppermute x4, waiting for transfers between devices, along_first(): return lax.ppermute(value, ('row', 'col'), device_pairs(move))  29.6 us
    all_to_all x1, blocking collectives, on_device(): own = lax.all_to_all(split, 'col', split_axis=1, concat_axis=1, tiled=True)  26.3 us
    ppermute x8, waiting for transfers between devices, along_second(): return lax.ppermute(value, ('row', 'col'), device_pairs(move))  22.5 us
    pallas_call x1, Pallas kernels, late_product(): pl.pallas_call(late_kernel, out_shape=[jax.ShapeDtypeStruct((pairs // 2,...  19.4 us
    select_n x1, other arithmetic, on_device(): jnp.where(row_irrep[:, None] == col_irrep[None, :], hole_panel, jnp.zeros...  11.6 us
    ppermute x8, starting transfers between devices, along_second(): return lax.ppermute(value, ('row', 'col'), device_pairs(move))  11.4 us
    ppermute x3, waiting for transfers between devices, along_y(): lax.ppermute(value, ('row', 'col'), device_pairs(lambda x, z, y, core: (x...  9.13 us
  transfers between devices with their start and end apart: 16, of which 7 were waited for; matrix products, arithmetic and copies ran while one was open for 18% of the time, Pallas kernels for 15%

profile of v1, /device:TPU:6, one launch (start us, length us, event | category | flops | bytes accessed | tf_op | source)
XLA Modules:
  0.0 199.8 jit_solution(16784292644589753151)
XLA Ops:
  0.0 26.3 %all_to_all.5 = bf16[6,8,12288]{2,0,1:T(8,128)(2,1)S(1)} all-to-all(bf16[6,8,12288]{2,0,1:T(8,128)(2,1)} %bitcast.16), channel_id=1, replica_groups=mesh['row'=16,'col'=8] {'col'}, dimensions={1} | all-to-all | bytes 2359296 | tf_op jit(solution)/shard_map/all_to_all | solution.py:202
  26.3 0.7 copy.21
  26.9 0.0 copy-start.5
  26.9 0.0 copy-start.6
  27.0 0.5 collective-permute-start
  27.5 1.5 collective-permute-start.1
  29.0 14.2 %collective-permute-done = bf16[48,12288]{1,0:T(8,128)(2,1)S(1)} collective-permute-done((bf16[48,12288]{1,0:T(8,128)(2,1)S(1)}, bf16[48,12288]{1,0:T(8,128)(2,1)S(1)}, u32[]{:S(2)}, u32[]{:S(2)}) %collective-permute-start) | collective-permute-done | bytes 1179680 | tf_op jit(solution)/shard_map/ppermute | solution.py:39
  43.2 1.7 collective-permute-done.1
  44.9 0.3 pad_maximum_fusion.refs_0_
  45.2 0.7 copy-done.1
  46.0 1.9 collective-permute-start.2
  47.9 2.1 %collective-permute-start.4 = (bf16[144,12288]{1,0:T(8,128)(2,1)S(1)}, bf16[144,12288]{1,0:T(8,128)(2,1)}, u32[]{:S(2)}, u32[]{:S(2)}) collective-permute-start(bf16[144,12288]{1,0:T(8,128)(2,1)S(1)} %pad_maximum_fusion.refs_0_), channel_id=1, source_target_pairs={{0,24},{1,97},{2,26},{3,99},{4,28},{5,101},{6,30},{7,103},{8,0},{9... | collective-permute-start | bytes 10616840 | tf_op jit(solution)/shard_map/ppermute | solution.py:45
  50.0 0.9 slice.50
  50.9 0.3 collective-permute-start.6
  51.2 0.2 reduce-window.17
  51.3 0.2 reduce-window.16
  51.5 0.1 convert_reduce_fusion.1
  51.6 0.2 convert_reduce_fusion
  51.8 1.1 slice.51
  52.9 1.8 collective-permute-start.7
  54.7 12.7 %collective-permute-done.6 = bf16[48,6144]{1,0:T(8,128)(2,1)} collective-permute-done((bf16[48,6144]{1,0:T(8,128)(2,1)}, bf16[48,6144]{1,0:T(8,128)(2,1)}, u32[]{:S(2)}, u32[]{:S(2)}) %collective-permute-start.6) | collective-permute-done | bytes 589856 | tf_op jit(solution)/shard_map/ppermute | solution.py:39
  67.5 2.0 constant_dynamic-update-slice_fusion.1
  69.4 1.1 collective-permute-done.7
  70.5 0.9 constant_dynamic-update-slice_fusion.refs_1_
  71.3 2.0 %collective-permute-start.10 = (bf16[48,12288]{1,0:T(8,128)(2,1)}, bf16[48,12288]{1,0:T(8,128)(2,1)}, u32[]{:S(2)}, u32[]{:S(2)}) collective-permute-start(bf16[48,12288]{1,0:T(8,128)(2,1)} %constant_dynamic-update-slice_fusion.refs_1_), channel_id=1, source_target_pairs={{0,24},{1,97},{2,26},{3,99},{4,28},{5,101},{6,30},{7,103},{8,0},{9... | collective-permute-start | bytes 3538952 | tf_op jit(solution)/shard_map/ppermute | solution.py:45
  73.3 22.5 %collective-permute-done.2.refs_2_ = bf16[144,12288]{1,0:T(8,128)(2,1)} collective-permute-done((bf16[144,12288]{1,0:T(8,128)(2,1)S(1)}, bf16[144,12288]{1,0:T(8,128)(2,1)}, u32[]{:S(2)}, u32[]{:S(2)}) %collective-permute-start.2) | collective-permute-done | bytes 3538976 | tf_op jit(solution)/shard_map/ppermute | solution.py:45
  95.9 2.9 %slice.48 = bf16[72,12288]{1,0:T(8,128)(2,1)} slice(bf16[144,12288]{1,0:T(8,128)(2,1)} %collective-permute-done.2.refs_2_), slice={[0:72], [0:12288]} | slice | bytes 3538944 | tf_op jit(solution)/shard_map/slice | solution.py:220
  98.7 1.6 slice.49
  100.3 0.0 copy-start.3
  100.3 3.3 %collective-permute-start.5 = (bf16[72,12288]{1,0:T(8,128)(2,1)S(1)}, bf16[72,12288]{1,0:T(8,128)(2,1)S(1)}, u32[]{:S(2)}, u32[]{:S(2)}) collective-permute-start(bf16[72,12288]{1,0:T(8,128)(2,1)S(1)} %slice.49), channel_id=1, source_target_pairs={{0,24},{1,97},{2,26},{3,99},{4,28},{5,101},{6,30},{7,103},{8,0},{9... | collective-permute-start | bytes 5308424 | tf_op jit(solution)/shard_map/ppermute | solution.py:45
  103.6 11.6 %compare_select_fusion.panel_ref = bf16[512,12288]{1,0:T(8,128)(2,1)} fusion(bf16[512,12288]{1,0:T(8,128)(2,1)} %param.9, s32[12288]{0:T(1024)S(1)} %convert_reduce_fusion, s32[512]{0:T(512)S(1)} %convert_reduce_fusion.1), kind=kLoop, calls=%fused_computation.4 | loop fusion | flops 12582912 | bytes 25217024 | tf_op jit(solution)/shard_map/jit(_where)/select_n | solution.py:207
  115.3 0.0 collective-permute-done.10.refs_5_
  115.3 2.0 slice.53
  117.2 0.6 collective-permute-start.11
  117.9 0.0 collective-permute-done.8.refs_3_
  117.9 1.9 slice.52
  119.8 1.4 collective-permute-start.9
  121.2 0.5 broadcast_or_fusion.2
  121.7 0.8 reshape.82
  122.5 1.6 copy.16
  124.1 0.9 reshape.83
  125.0 0.5 broadcast_or_fusion.1
  125.6 0.7 gather_fusion.2
  126.3 0.1 reshape.92
  126.4 0.7 gather_fusion.3
  127.1 0.6 reshape.93
  127.7 0.7 gather_fusion.1
  128.4 0.7 reshape.91
  129.0 0.7 gather_fusion
  129.7 0.7 reshape.84.place_ref
  130.4 1.3 pad_add_fusion.place_ref
  131.7 30.3 %early_product.1.early_ref = f32[768,512]{1,0:T(8,128)} custom-call(s32[576]{0:T(1024)} %pad_add_fusion.place_ref, bf16[512,12288]{1,0:T(8,128)(2,1)} %compare_select_fusion.panel_ref, bf16[144,12288]{1,0:T(8,128)(2,1)} %copy-done, bf16[48,12288]{1,0:T(8,128)(2,1)} %constant_dynamic-update-slice_fusion.refs_1_, ...), custom_call_target="tpu_custom_call" | custom-call | tf_op jit(solution)/shard_map/early_product/pallas_call | solution.py:97
  162.1 0.0 collective-permute-done.11.right_ref
  162.1 0.0 collective-permute-done.9.left_ref
  162.1 0.0 collective-permute-done.5.high_ref
  162.1 1.2 copy-done.2
  163.4 19.4 %late_product.1 = (f32[384,512]{1,0:T(8,128)}, f32[384,512]{1,0:T(8,128)}) custom-call(s32[192]{0:T(256)} %reshape.84.place_ref, bf16[512,12288]{1,0:T(8,128)(2,1)} %compare_select_fusion.panel_ref, bf16[72,12288]{1,0:T(8,128)(2,1)} %collective-permute-done.3.low_ref, bf16[72,12288]{1,0:T(8,128)(2,1)} %copy-done.2, ...), custom_call_target="tpu_custom_call" | custom-call | tf_op jit(solution)/shard_map/late_product/pallas_call | solution.py:153
  182.8 0.0 collective-permute-start.12
  182.8 2.5 %collective-permute-done.12 = f32[384,512]{1,0:T(8,128)S(1)} collective-permute-done((f32[384,512]{1,0:T(8,128)}, f32[384,512]{1,0:T(8,128)S(1)}, u32[]{:S(2)}, u32[]{:S(2)}) %collective-permute-start.12) | collective-permute-done | bytes 786464 | tf_op jit(solution)/shard_map/ppermute | solution.py:55
  185.3 1.3 add.155
  186.6 0.6 collective-permute-start.13
  187.2 2.7 %collective-permute-start.14 = (f32[96,512]{1,0:T(8,128)S(1)}, f32[96,512]{1,0:T(8,128)S(1)}, u32[]{:S(2)}, u32[]{:S(2)}) collective-permute-start(f32[96,512]{1,0:T(8,128)S(1)} %get-tuple-element.13), channel_id=1, source_target_pairs={{0,6},{1,7},{2,0},{3,1},{4,2},{5,3},{6,4},{7,5},{8,14},{9,15},{10,... | collective-permute-start | bytes 589832 | tf_op jit(solution)/shard_map/ppermute | solution.py:49
  189.9 9.1 %collective-permute-done.13 = f32[96,512]{1,0:T(8,128)S(1)} collective-permute-done((f32[96,512]{1,0:T(8,128)S(1)}, f32[96,512]{1,0:T(8,128)S(1)}, u32[]{:S(2)}, u32[]{:S(2)}) %collective-permute-start.13) | collective-permute-done | bytes 196640 | tf_op jit(solution)/shard_map/ppermute | solution.py:49
  199.0 0.7 fusion.2
  (21 shorter events, 0.1 us)
Async XLA Ops:
  26.9 24.2 %copy-start.5 = (s32[8]{0:T(128)S(1)}, s32[8]{0:T(128)}, u32[]{:S(2)}) copy-start(s32[8]{0:T(128)} %param.12) | copy-start | bytes 100
  26.9 24.4 %copy-start.6 = (s32[8]{0:T(128)S(1)}, s32[8]{0:T(128)}, u32[]{:S(2)}) copy-start(s32[8]{0:T(128)} %param.11) | copy-start | bytes 100
  27.0 16.3 %collective-permute-start = (bf16[48,12288]{1,0:T(8,128)(2,1)S(1)}, bf16[48,12288]{1,0:T(8,128)(2,1)S(1)}, u32[]{:S(2)}, u32[]{:S(2)}) collective-permute-start(bf16[48,12288]{1,0:T(8,128)(2,1)S(1)} %bitcast.13), channel_id=1, source_target_pairs={{0,32},{1,9},{2,34},{3,11},{4,36},{5,13},{6,38},{7,15},{8,40},{9,1... | collective-permute-start | bytes 3538952 | tf_op jit(solution)/shard_map/ppermute | solution.py:39
  27.5 17.4 %collective-permute-start.1 = (bf16[48,12288]{1,0:T(8,128)(2,1)S(1)}, bf16[48,12288]{1,0:T(8,128)(2,1)S(1)}, u32[]{:S(2)}, u32[]{:S(2)}) collective-permute-start(bf16[48,12288]{1,0:T(8,128)(2,1)S(1)} %bitcast.14), channel_id=1, source_target_pairs={{0,96},{1,25},{2,98},{3,27},{4,100},{5,29},{6,102},{7,31},{8,104},... | collective-permute-start | bytes 3538952 | tf_op jit(solution)/shard_map/ppermute | solution.py:39
  44.9 1.0 copy-start.1
  45.9 23.5 %copy-start = (bf16[144,12288]{1,0:T(8,128)(2,1)}, bf16[144,12288]{1,0:T(8,128)(2,1)S(1)}, u32[]{:S(2)}) copy-start(bf16[144,12288]{1,0:T(8,128)(2,1)S(1)} %pad_maximum_fusion.refs_0_) | copy-start | bytes 10616836
  46.0 49.9 %collective-permute-start.2 = (bf16[144,12288]{1,0:T(8,128)(2,1)S(1)}, bf16[144,12288]{1,0:T(8,128)(2,1)}, u32[]{:S(2)}, u32[]{:S(2)}) collective-permute-start(bf16[144,12288]{1,0:T(8,128)(2,1)S(1)} %pad_maximum_fusion.refs_0_), channel_id=1, source_target_pairs={{0,8},{1,33},{2,10},{3,35},{4,12},{5,37},{6,14},{7,39},{8,16},{9,4... | collective-permute-start | bytes 10616840 | tf_op jit(solution)/shard_map/ppermute | solution.py:45
  47.9 50.9 %collective-permute-start.4 = (bf16[144,12288]{1,0:T(8,128)(2,1)S(1)}, bf16[144,12288]{1,0:T(8,128)(2,1)}, u32[]{:S(2)}, u32[]{:S(2)}) collective-permute-start(bf16[144,12288]{1,0:T(8,128)(2,1)S(1)} %pad_maximum_fusion.refs_0_), channel_id=1, source_target_pairs={{0,24},{1,97},{2,26},{3,99},{4,28},{5,101},{6,30},{7,103},{8,0},{9... | collective-permute-start | bytes 10616840 | tf_op jit(solution)/shard_map/ppermute | solution.py:45
  50.9 16.6 %collective-permute-start.6 = (bf16[48,6144]{1,0:T(8,128)(2,1)}, bf16[48,6144]{1,0:T(8,128)(2,1)}, u32[]{:S(2)}, u32[]{:S(2)}) collective-permute-start(bf16[48,6144]{1,0:T(8,128)(2,1)} %slice.50), channel_id=1, source_target_pairs={{0,32},{1,9},{2,34},{3,11},{4,36},{5,13},{6,38},{7,15},{8,40},{9,1... | collective-permute-start | bytes 1769480 | tf_op jit(solution)/shard_map/ppermute | solution.py:39
  52.9 17.5 %collective-permute-start.7 = (bf16[48,6144]{1,0:T(8,128)(2,1)S(1)}, bf16[48,6144]{1,0:T(8,128)(2,1)S(1)}, u32[]{:S(2)}, u32[]{:S(2)}) collective-permute-start(bf16[48,6144]{1,0:T(8,128)(2,1)S(1)} %slice.51), channel_id=1, source_target_pairs={{0,96},{1,25},{2,98},{3,27},{4,100},{5,29},{6,102},{7,31},{8,104},... | collective-permute-start | bytes 1769480 | tf_op jit(solution)/shard_map/ppermute | solution.py:39
  71.3 44.0 %collective-permute-start.10 = (bf16[48,12288]{1,0:T(8,128)(2,1)}, bf16[48,12288]{1,0:T(8,128)(2,1)}, u32[]{:S(2)}, u32[]{:S(2)}) collective-permute-start(bf16[48,12288]{1,0:T(8,128)(2,1)} %constant_dynamic-update-slice_fusion.refs_1_), channel_id=1, source_target_pairs={{0,24},{1,97},{2,26},{3,99},{4,28},{5,101},{6,30},{7,103},{8,0},{9... | collective-permute-start | bytes 3538952 | tf_op jit(solution)/shard_map/ppermute | solution.py:45
  73.3 44.5 %collective-permute-start.8 = (bf16[48,12288]{1,0:T(8,128)(2,1)}, bf16[48,12288]{1,0:T(8,128)(2,1)}, u32[]{:S(2)}, u32[]{:S(2)}) collective-permute-start(bf16[48,12288]{1,0:T(8,128)(2,1)} %constant_dynamic-update-slice_fusion.refs_1_), channel_id=1, source_target_pairs={{0,8},{1,33},{2,10},{3,35},{4,12},{5,37},{6,14},{7,39},{8,16},{9,4... | collective-permute-start | bytes 3538952 | tf_op jit(solution)/shard_map/ppermute | solution.py:45
  98.7 63.4 %collective-permute-start.3 = (bf16[72,12288]{1,0:T(8,128)(2,1)}, bf16[72,12288]{1,0:T(8,128)(2,1)}, u32[]{:S(2)}, u32[]{:S(2)}) collective-permute-start(bf16[72,12288]{1,0:T(8,128)(2,1)} %slice.48), channel_id=1, source_target_pairs={{0,8},{1,33},{2,10},{3,35},{4,12},{5,37},{6,14},{7,39},{8,16},{9,4... | collective-permute-start | bytes 5308424 | tf_op jit(solution)/shard_map/ppermute | solution.py:45
  100.3 14.9 %copy-start.3 = (s32[768]{0:T(1024)S(1)}, s32[768]{0:T(1024)}, u32[]{:S(2)}) copy-start(s32[768]{0:T(1024)} %param.13) | copy-start | bytes 9220
  100.3 61.8 %collective-permute-start.5 = (bf16[72,12288]{1,0:T(8,128)(2,1)S(1)}, bf16[72,12288]{1,0:T(8,128)(2,1)S(1)}, u32[]{:S(2)}, u32[]{:S(2)}) collective-permute-start(bf16[72,12288]{1,0:T(8,128)(2,1)S(1)} %slice.49), channel_id=1, source_target_pairs={{0,24},{1,97},{2,26},{3,99},{4,28},{5,101},{6,30},{7,103},{8,0},{9... | collective-permute-start | bytes 5308424 | tf_op jit(solution)/shard_map/ppermute | solution.py:45
  115.2 5.9 %copy-start.4 = (s32[4]{0:T(128)S(1)}, s32[4]{0:T(128)}, u32[]{:S(2)}) copy-start(s32[4]{0:T(128)} %constant.158) | copy-start | bytes 52
  117.2 44.9 %collective-permute-start.11 = (bf16[48,6144]{1,0:T(8,128)(2,1)}, bf16[48,6144]{1,0:T(8,128)(2,1)}, u32[]{:S(2)}, u32[]{:S(2)}) collective-permute-start(bf16[48,6144]{1,0:T(8,128)(2,1)} %slice.53), channel_id=1, source_target_pairs={{0,24},{1,97},{2,26},{3,99},{4,28},{5,101},{6,30},{7,103},{8,0},{9... | collective-permute-start | bytes 1769480 | tf_op jit(solution)/shard_map/ppermute | solution.py:45
  119.8 42.3 %collective-permute-start.9 = (bf16[48,6144]{1,0:T(8,128)(2,1)}, bf16[48,6144]{1,0:T(8,128)(2,1)}, u32[]{:S(2)}, u32[]{:S(2)}) collective-permute-start(bf16[48,6144]{1,0:T(8,128)(2,1)} %slice.52), channel_id=1, source_target_pairs={{0,8},{1,33},{2,10},{3,35},{4,12},{5,37},{6,14},{7,39},{8,16},{9,4... | collective-permute-start | bytes 1769480 | tf_op jit(solution)/shard_map/ppermute | solution.py:45
  162.1 1.2 copy-start.2
  182.8 2.5 %collective-permute-start.12 = (f32[384,512]{1,0:T(8,128)}, f32[384,512]{1,0:T(8,128)S(1)}, u32[]{:S(2)}, u32[]{:S(2)}) collective-permute-start(f32[384,512]{1,0:T(8,128)} %get-tuple-element.8), channel_id=1, source_target_pairs={{0,1},{1,0},{2,3},{3,2},{4,5},{5,4},{6,7},{7,6},{8,9},{9,8},{10,11... | collective-permute-start | bytes 2359304 | tf_op jit(solution)/shard_map/ppermute | solution.py:55
  186.6 12.4 %collective-permute-start.13 = (f32[96,512]{1,0:T(8,128)S(1)}, f32[96,512]{1,0:T(8,128)S(1)}, u32[]{:S(2)}, u32[]{:S(2)}) collective-permute-start(f32[96,512]{1,0:T(8,128)S(1)} %get-tuple-element.11), channel_id=1, source_target_pairs={{0,2},{1,3},{2,4},{3,5},{4,6},{5,7},{6,0},{7,1},{8,10},{9,11},{10,... | collective-permute-start | bytes 589832 | tf_op jit(solution)/shard_map/ppermute | solution.py:49
  187.2 11.8 %collective-permute-start.14 = (f32[96,512]{1,0:T(8,128)S(1)}, f32[96,512]{1,0:T(8,128)S(1)}, u32[]{:S(2)}, u32[]{:S(2)}) collective-permute-start(f32[96,512]{1,0:T(8,128)S(1)} %get-tuple-element.13), channel_id=1, source_target_pairs={{0,6},{1,7},{2,0},{3,1},{4,2},{5,3},{6,4},{7,5},{8,14},{9,15},{10,... | collective-permute-start | bytes 589832 | tf_op jit(solution)/shard_map/ppermute | solution.py:49
  189.9 9.1 %collective-permute-start.15 = (f32[96,512]{1,0:T(8,128)S(1)}, f32[96,512]{1,0:T(8,128)S(1)}, u32[]{:S(2)}, u32[]{:S(2)}) collective-permute-start(f32[96,512]{1,0:T(8,128)S(1)} %get-tuple-element.12), channel_id=1, source_target_pairs={{0,4},{1,5},{2,6},{3,7},{4,0},{5,1},{6,2},{7,3},{8,12},{9,13},{10,... | collective-permute-start | bytes 589832 | tf_op jit(solution)/shard_map/ppermute | solution.py:49

commit v2 on v0

v2 whole, which is shorter than its diff:
```python
import functools

import jax
import jax.numpy as jnp
from jax import lax
from jax.experimental import pallas as pl
from jax.experimental.pallas import tpu as pltpu
from jax.sharding import PartitionSpec as P

SIDE = 4
CORES = 2
BLOCK = 3072


def irrep_labels(sizes, count, offset):
    position = offset + lax.iota(jnp.int32, count)
    bounds = jnp.cumsum(sizes)
    return jnp.sum((position[:, None] >= bounds[None, :]).astype(jnp.int32), axis=1)


def device_pairs(move):
    pairs = []
    for x in range(SIDE):
        for z in range(SIDE):
            for y in range(SIDE):
                for core in range(CORES):
                    to_x, to_z, to_y, to_core = move(x, z, y, core)
                    to = (to_x % SIDE) * SIDE + to_z % SIDE
                    pairs.append((
                        ((x * SIDE + z) * SIDE + y) * CORES + core,
                        (to * SIDE + to_y % SIDE) * CORES + to_core % CORES,
                    ))
    return pairs


def along_first(value, step):
    def move(x, z, y, core):
        return (x + step, z, y, core) if core == 0 else (x, z + step, y, core)
    return lax.ppermute(value, ("row", "col"), device_pairs(move))


def along_second(value, step):
    def move(x, z, y, core):
        return (x, z + step, y, core) if core == 0 else (x + step, z, y, core)
    return lax.ppermute(value, ("row", "col"), device_pairs(move))


def along_y(value, step):
    return lax.ppermute(
        value, ("row", "col"), device_pairs(lambda x, z, y, core: (x, z, y + step, core))
    )


def to_other_core(value):
    return lax.ppermute(
        value, ("row", "col"), device_pairs(lambda x, z, y, core: (x, z, y, core + 1))
    )


def product(piece, panel):
    numbers = (((1,), (1,)), ((), ()))
    return lax.dot_general(piece, panel, numbers, preferred_element_type=jnp.float32)


def place_rows(goes_ref, base_ref, total_ref, out_ref, units, per_device):
    unit = total_ref.shape[0] // units
    group = unit // per_device

    def body(index, carry):
        base = base_ref[index]
        for pair in range(per_device):
            at = pl.multiple_of(index * unit + pair * group, group)
            rows = total_ref[pl.ds(at, group), :]
            for device in range(group):
                goes = goes_ref[base + device * per_device + pair]
                out_ref[pl.ds(goes, 1), :] = rows[device:device + 1, :]
        return carry
    lax.fori_loop(0, units, body, 0)


def join(piece_refs, joined_ref):
    at = 0
    for piece_ref in piece_refs:
        joined_ref[pl.ds(at, piece_ref.shape[0]), :] = piece_ref[...]
        at += piece_ref.shape[0]


def early_kernel(per_device, goes_ref, base_ref, panel_ref, *refs):
    *piece_refs, out_ref, total_ref, joined_ref = refs
    step = pl.program_id(0)

    @pl.when(step == 0)
    def _():
        total_ref[...] = jnp.zeros_like(total_ref)

    join(piece_refs, joined_ref)
    total_ref[...] += product(joined_ref[...], panel_ref[...])

    @pl.when(step == pl.num_programs(0) - 1)
    def _():
        units = SIDE * (SIDE - 1)
        place_rows(goes_ref, base_ref, total_ref, out_ref, units, per_device)


def late_kernel(per_device, goes_ref, base_ref, panel_ref, *refs):
    *piece_refs, early_ref, mine_ref, theirs_ref, total_ref, all_ref, joined_ref = refs
    step = pl.program_id(0)

    @pl.when(step == 0)
    def _():
        total_ref[...] = jnp.zeros_like(total_ref)
        all_ref[...] = early_ref[...]

    join(piece_refs, joined_ref)
    total_ref[...] += product(joined_ref[...], panel_ref[...])

    @pl.when(step == pl.num_programs(0) - 1)
    def _():
        place_rows(goes_ref, base_ref, total_ref, all_ref, SIDE, per_device)
        half = mine_ref.shape[0]
        mine_ref[...] = all_ref[pl.ds(0, half), :]
        theirs_ref[...] = all_ref[pl.ds(half, half), :]


def by_step(height):
    return pl.BlockSpec((height, BLOCK), lambda k, goes, bases: (0, k))


def at_once(height, rows):
    return pl.BlockSpec((height, rows), lambda k, goes, bases: (0, 0))


def early_product(goes, bases, panel, pieces, per_device):
    rows, depth = panel.shape
    pairs = goes.shape[0]
    count = sum(piece.shape[0] for piece in pieces)
    return pl.pallas_call(
        functools.partial(early_kernel, per_device),
        out_shape=jax.ShapeDtypeStruct((pairs, rows), jnp.float32),
        grid_spec=pltpu.PrefetchScalarGridSpec(
            num_scalar_prefetch=2,
            grid=(depth // BLOCK,),
            in_specs=[by_step(value.shape[0]) for value in (panel, *pieces)],
            out_specs=at_once(pairs, rows),
            scratch_shapes=[pltpu.VMEM((count, rows), jnp.float32),
                            pltpu.VMEM((count, BLOCK), panel.dtype)],
        ),
        name="early_product",
    )(goes, bases, panel, *pieces)


def late_product(goes, bases, panel, pieces, early, per_device):
    rows, depth = panel.shape
    pairs = early.shape[0]
    count = sum(piece.shape[0] for piece in pieces)
    return pl.pallas_call(
        functools.partial(late_kernel, per_device),
        out_shape=[jax.ShapeDtypeStruct((pairs // 2, rows), jnp.float32)] * 2,
        grid_spec=pltpu.PrefetchScalarGridSpec(
            num_scalar_prefetch=2,
            grid=(depth // BLOCK,),
            in_specs=[by_step(value.shape[0]) for value in (panel, *pieces)]
            + [at_once(pairs, rows)],
            out_specs=[at_once(pairs // 2, rows)] * 2,
            scratch_shapes=[pltpu.VMEM((count, rows), jnp.float32),
                            pltpu.VMEM((pairs, rows), jnp.float32),
                            pltpu.VMEM((count, BLOCK), panel.dtype)],
        ),
        name="late_product",
    )(goes, bases, panel, *pieces, early)


def gather_units(own):
    unit = own.shape[0]
    half, cut = unit // 2, unit + unit // 2
    back, ahead = along_first(own, 1), along_first(own, -1)
    far = jnp.concatenate([along_first(back[:half], 1), along_first(ahead[half:], -1)], axis=0)
    near = jnp.concatenate([own, back, ahead], axis=0)
    near_1, near_3 = along_second(near, 1), along_second(near, -1)
    far_1, far_3 = along_second(far, 1), along_second(far, -1)
    late = (
        along_second(near_1[:cut], 1), along_second(near_3[cut:], -1),
        along_second(far_1[:half], 1), along_second(far_3[half:], -1),
    )
    return (near, far, near_1, far_1, near_3, far_3), late


def on_device(hole_panel, amplitudes, row_sizes, col_sizes, pair_order):
    row_count, col_count = hole_panel.shape
    col_devices = lax.axis_size("col")
    per_device = amplitudes.shape[0]
    unit = per_device * col_devices
    row_at, col_at = lax.axis_index("row"), lax.axis_index("col")
    my_x, my_z = row_at // SIDE, row_at % SIDE
    my_y, my_core = col_at // CORES, col_at % CORES

    split = amplitudes.reshape(per_device, col_devices, col_count)
    own = lax.all_to_all(split, "col", split_axis=1, concat_axis=1, tiled=True)
    own = own.reshape(unit, col_count)

    row_irrep = irrep_labels(row_sizes, row_count, row_at * row_count)
    col_irrep = irrep_labels(col_sizes, col_count, col_at * col_count)
    masked = jnp.where(
        row_irrep[:, None] == col_irrep[None, :], hole_panel, jnp.zeros((), hole_panel.dtype)
    )
    own, masked = lax.optimization_barrier((own, masked))

    out_pairs = pair_order.shape[0] // col_devices
    owner = pair_order // out_pairs
    block = (owner // CORES - my_y) % SIDE + SIDE * ((owner - my_core) % CORES)
    goes = (block * out_pairs + pair_order % out_pairs).astype(jnp.int32)
    second_hop, first_hop = jnp.array([0, 1, 3, 2])[:, None], jnp.array([0, 1, 3, 2])[None, :]
    unit_x = my_x - jnp.where(my_core == 0, first_hop, second_hop)
    unit_z = my_z - jnp.where(my_core == 0, second_hop, first_hop)
    bases = ((unit_x % SIDE) * SIDE + unit_z % SIDE).reshape(-1).astype(jnp.int32) * unit
    early_bases, late_bases = bases[:SIDE * (SIDE - 1)], bases[SIDE * (SIDE - 1):]

    early_pieces, late_pieces = gather_units(own)
    early = early_product(goes, early_bases, masked, early_pieces, per_device)
    mine, theirs = late_product(goes, late_bases, masked, late_pieces, early, per_device)
    shares = mine + to_other_core(theirs)
    total = shares[:out_pairs]
    for hop in (1, 3, 2):
        total = total + along_y(shares[hop * out_pairs:(hop + 1) * out_pairs], hop)
    return total.T


def solution(mesh):
    in_specs = (P("row", "col"), P(("row", "col"), None), P(), P(), P())
    out_specs = P("row", "col")
    return jax.shard_map(
        on_device, mesh=mesh, in_specs=in_specs, out_specs=out_specs, check_vma=False
    )
```

time: 221 us -> 163 us (0.74)
  waiting for transfers between devices: 154 us -> 82.6 us
  Pallas kernels: 0 us -> 26.7 us
  blocking collectives: 26.3 us -> 0 us
  starting transfers between devices: 0.04 us -> 24.9 us
  matrix products: 17.6 us -> 0 us
  other arithmetic: 0.65 us -> 15 us
  between operations: 13.5 us -> 0.13 us
  local copies, waits for them, and re-layouts: 8.5 us -> 12.6 us
    all_gather x1 -> x0, waiting for transfers between devices: 122 us -> none  [on_device(): lax.all_gather(split_rows, 'row', axis=0, tiled=True)]
    ppermute x0 -> x16, waiting for transfers between devices: none -> 73.3 us  [the longest x8 31.1 us: along_second(): return lax.ppermute(value, ('row', 'col'), device_pairs(move))]
    reduce_scatter x1 -> x0, waiting for transfers between devices: 32.5 us -> none  [on_device(): return lax.psum_scatter(logical, 'col', scatter_dimension=1, tiled=True)]
    pallas_call x0 -> x2, Pallas kernels: none -> 26.7 us  [the longest x1 15.1 us: early_product(): pl.pallas_call(functools.partial(early_kernel, per_device), out_shape=jax...]
    all_to_all x1 -> x0, blocking collectives: 26.3 us -> none  [on_device(): lax.all_to_all(amplitudes, 'col', split_axis=1, concat_axis=0, tiled=True)]
    ppermute x0 -> x16, starting transfers between devices: none -> 20.3 us  [the longest x8 12.7 us: along_second(): return lax.ppermute(value, ('row', 'col'), device_pairs(move))]
    dot_general x1 -> x0, matrix products: 17.6 us -> none  [contract(): lax.dot_general(masked, piece, numbers, preferred_element_type=jnp.float32)]
    select_n x1, other arithmetic: 0.01 us -> 11.6 us  [on_device(): jnp.where(row_irrep[:, None] == col_irrep[None, :], hole_panel, jnp.zeros...]
  transfers between devices with their start and end apart: 2 -> 17, of which waited for: 2 -> 11; matrix products, arithmetic and copies ran while one was open for 0% -> 13% of each run, Pallas kernels for 0% -> 9%
where the time goes in v2:
time: 163 us; the launch traced here: 162 us
  waiting for transfers between devices  82.6 us (51%)
  Pallas kernels  26.7 us (16%)
  starting transfers between devices  24.9 us (15%)
  other arithmetic  15 us (9%)
  local copies, waits for them, and re-layouts  12.6 us (8%)
    ppermute x8, waiting for transfers between devices, along_second(): return lax.ppermute(value, ('row', 'col'), device_pairs(move))  31.1 us
    ppermute x4, waiting for transfers between devices, along_first(): return lax.ppermute(value, ('row', 'col'), device_pairs(move))  30.6 us
    pallas_call x1, Pallas kernels, early_product(): pl.pallas_call(functools.partial(early_kernel, per_device), out_shape=jax...  15.1 us
    ppermute x8, starting transfers between devices, along_second(): return lax.ppermute(value, ('row', 'col'), device_pairs(move))  12.7 us
    select_n x1, other arithmetic, on_device(): jnp.where(row_irrep[:, None] == col_irrep[None, :], hole_panel, jnp.zeros...  11.6 us
    pallas_call x1, Pallas kernels, late_product(): pl.pallas_call(functools.partial(late_kernel, per_device), out_shape=[jax...  11.6 us
    all_to_all x1, waiting for transfers between devices, on_device(): own = lax.all_to_all(split, 'col', split_axis=1, concat_axis=1, tiled=True)  9.27 us
    ppermute x3, waiting for transfers between devices, along_y(): lax.ppermute(value, ('row', 'col'), device_pairs(lambda x, z, y, core: (x...  9.13 us
  transfers between devices with their start and end apart: 17, of which 11 were waited for; matrix products, arithmetic and copies ran while one was open for 13% of the time, Pallas kernels for 9%

profile of v2, /device:TPU:6, one launch (start us, length us, event | category | flops | bytes accessed | tf_op | source)
XLA Modules:
  0.0 161.9 jit_solution(2008862771476109138)
XLA Ops:
  0.0 4.6 %all-to-all-start = ((bf16[6,8,12288]{2,0,1:T(8,128)(2,1)}), bf16[6,8,12288]{2,0,1:T(8,128)(2,1)S(1)}, u32[]{:S(2)}, u32[]{:S(2)}) async-start(bf16[6,8,12288]{2,0,1:T(8,128)(2,1)} %bitcast.14), calls=%async_computation | async-start | bytes 3145728 | tf_op jit(solution)/shard_map/all_to_all | solution.py:198
  4.6 0.0 copy-done.7
  4.6 0.2 reduce-window.17
  4.8 0.2 reduce-window.16
  5.0 0.2 convert_reduce_fusion
  5.2 0.1 convert_reduce_fusion.1
  5.3 11.6 %compare_select_fusion.panel_ref = bf16[512,12288]{1,0:T(8,128)(2,1)} fusion(bf16[512,12288]{1,0:T(8,128)(2,1)} %param.7, s32[12288]{0:T(1024)S(1)} %convert_reduce_fusion, s32[512]{0:T(512)S(1)} %convert_reduce_fusion.1), kind=kLoop, calls=%fused_computation | loop fusion | flops 12582912 | bytes 25217024 | tf_op jit(solution)/shard_map/jit(_where)/select_n | solution.py:203
  16.9 9.3 %all-to-all-done = bf16[6,8,12288]{2,0,1:T(8,128)(2,1)S(1)} async-done(((bf16[6,8,12288]{2,0,1:T(8,128)(2,1)}), bf16[6,8,12288]{2,0,1:T(8,128)(2,1)S(1)}, u32[]{:S(2)}, u32[]{:S(2)}) %all-to-all-start) | async-done | bytes 1179680 | tf_op jit(solution)/shard_map/all_to_all | solution.py:198
  26.2 0.7 copy.11
  26.8 0.5 collective-permute-start
  27.4 1.5 collective-permute-start.1
  28.9 0.1 constant_dynamic-update-slice_fusion.2
  29.0 14.1 %collective-permute-done = bf16[48,12288]{1,0:T(8,128)(2,1)S(1)} collective-permute-done((bf16[48,12288]{1,0:T(8,128)(2,1)S(1)}, bf16[48,12288]{1,0:T(8,128)(2,1)S(1)}, u32[]{:S(2)}, u32[]{:S(2)}) %collective-permute-start) | collective-permute-done | bytes 1179680 | tf_op jit(solution)/shard_map/ppermute | solution.py:39
  43.1 0.1 constant_dynamic-update-slice_fusion.1
  43.2 1.6 collective-permute-done.1
  44.8 0.1 constant_dynamic-update-slice_fusion.refs_0_
  44.9 2.0 %collective-permute-start.2 = (bf16[144,12288]{1,0:T(8,128)(2,1)S(1)}, bf16[144,12288]{1,0:T(8,128)(2,1)S(1)}, u32[]{:S(2)}, u32[]{:S(2)}) collective-permute-start(bf16[144,12288]{1,0:T(8,128)(2,1)S(1)} %constant_dynamic-update-slice_fusion.refs_0_), channel_id=1, source_target_pairs={{0,8},{1,33},{2,10},{3,35},{4,12},{5,37},{6,14},{7,39},{8,16},{9,4... | collective-permute-start | bytes 10616840 | tf_op jit(solution)/shard_map/ppermute | solution.py:45
  46.9 2.2 %collective-permute-start.4 = (bf16[144,12288]{1,0:T(8,128)(2,1)S(1)}, bf16[144,12288]{1,0:T(8,128)(2,1)S(1)}, u32[]{:S(2)}, u32[]{:S(2)}) collective-permute-start(bf16[144,12288]{1,0:T(8,128)(2,1)S(1)} %constant_dynamic-update-slice_fusion.refs_0_), channel_id=1, source_target_pairs={{0,24},{1,97},{2,26},{3,99},{4,28},{5,101},{6,30},{7,103},{8,0},{9... | collective-permute-start | bytes 10616840 | tf_op jit(solution)/shard_map/ppermute | solution.py:45
  49.1 0.3 collective-permute-start.6
  49.5 1.8 %collective-permute-start.7 = (bf16[24,12288]{1,0:T(8,128)(2,1)S(1)}, bf16[24,12288]{1,0:T(8,128)(2,1)S(1)}, u32[]{:S(2)}, u32[]{:S(2)}) collective-permute-start(bf16[24,12288]{1,0:T(8,128)(2,1)S(1)} %slice.51), channel_id=1, source_target_pairs={{0,96},{1,25},{2,98},{3,27},{4,100},{5,29},{6,102},{7,31},{8,104},... | collective-permute-start | bytes 1769480 | tf_op jit(solution)/shard_map/ppermute | solution.py:39
  51.3 14.1 %collective-permute-done.6 = bf16[24,12288]{1,0:T(8,128)(2,1)S(1)} collective-permute-done((bf16[24,12288]{1,0:T(8,128)(2,1)S(1)}, bf16[24,12288]{1,0:T(8,128)(2,1)S(1)}, u32[]{:S(2)}, u32[]{:S(2)}) %collective-permute-start.6) | collective-permute-done | bytes 589856 | tf_op jit(solution)/shard_map/ppermute | solution.py:39
  65.5 0.8 constant_dynamic-update-slice_fusion.4
  66.3 0.8 collective-permute-done.7
  67.1 0.9 constant_dynamic-update-slice_fusion.3.refs_1_
  67.9 1.9 %collective-permute-start.10 = (bf16[48,12288]{1,0:T(8,128)(2,1)}, bf16[48,12288]{1,0:T(8,128)(2,1)}, u32[]{:S(2)}, u32[]{:S(2)}) collective-permute-start(bf16[48,12288]{1,0:T(8,128)(2,1)} %constant_dynamic-update-slice_fusion.3.refs_1_), channel_id=1, source_target_pairs={{0,24},{1,97},{2,26},{3,99},{4,28},{5,101},{6,30},{7,103},{8,0},{9... | collective-permute-start | bytes 3538952 | tf_op jit(solution)/shard_map/ppermute | solution.py:45
  69.9 0.1 collective-permute-start.8
  70.0 24.1 %collective-permute-done.2.refs_2_ = bf16[144,12288]{1,0:T(8,128)(2,1)S(1)} collective-permute-done((bf16[144,12288]{1,0:T(8,128)(2,1)S(1)}, bf16[144,12288]{1,0:T(8,128)(2,1)S(1)}, u32[]{:S(2)}, u32[]{:S(2)}) %collective-permute-start.2) | collective-permute-done | bytes 3538976 | tf_op jit(solution)/shard_map/ppermute | solution.py:45
  94.1 1.5 slice.48
  95.6 0.8 copy-done
  96.4 0.0 collective-permute-start.3
  96.4 0.0 collective-permute-done.4.refs_4_
  96.4 0.1 slice.49
  96.5 1.7 %copy-done.1 = bf16[144,12288]{1,0:T(8,128)(2,1)} copy-done((bf16[144,12288]{1,0:T(8,128)(2,1)}, bf16[144,12288]{1,0:T(8,128)(2,1)S(1)}, u32[]{:S(2)}) %copy-start.1) | copy-done | bytes 3538968
  98.2 3.2 %collective-permute-start.5 = (bf16[72,12288]{1,0:T(8,128)(2,1)S(1)}, bf16[72,12288]{1,0:T(8,128)(2,1)S(1)}, u32[]{:S(2)}, u32[]{:S(2)}) collective-permute-start(bf16[72,12288]{1,0:T(8,128)(2,1)S(1)} %slice.49), channel_id=1, source_target_pairs={{0,24},{1,97},{2,26},{3,99},{4,28},{5,101},{6,30},{7,103},{8,0},{9... | collective-permute-start | bytes 5308424 | tf_op jit(solution)/shard_map/ppermute | solution.py:45
  101.4 5.2 %collective-permute-done.10.refs_5_ = bf16[48,12288]{1,0:T(8,128)(2,1)} collective-permute-done((bf16[48,12288]{1,0:T(8,128)(2,1)}, bf16[48,12288]{1,0:T(8,128)(2,1)}, u32[]{:S(2)}, u32[]{:S(2)}) %collective-permute-start.10) | collective-permute-done | bytes 1179680 | tf_op jit(solution)/shard_map/ppermute | solution.py:45
  106.6 1.9 %slice.53 = bf16[24,12288]{1,0:T(8,128)(2,1)} slice(bf16[48,12288]{1,0:T(8,128)(2,1)} %collective-permute-done.10.refs_5_), slice={[24:48], [0:12288]} | slice | bytes 1179648 | tf_op jit(solution)/shard_map/slice | solution.py:183
  108.5 3.3 %collective-permute-start.11 = (bf16[24,12288]{1,0:T(8,128)(2,1)}, bf16[24,12288]{1,0:T(8,128)(2,1)}, u32[]{:S(2)}, u32[]{:S(2)}) collective-permute-start(bf16[24,12288]{1,0:T(8,128)(2,1)} %slice.53), channel_id=1, source_target_pairs={{0,24},{1,97},{2,26},{3,99},{4,28},{5,101},{6,30},{7,103},{8,0},{9... | collective-permute-start | bytes 1769480 | tf_op jit(solution)/shard_map/ppermute | solution.py:45
  111.8 0.0 collective-permute-done.8.refs_3_
  111.8 1.9 %slice.52 = bf16[24,12288]{1,0:T(8,128)(2,1)} slice(bf16[48,12288]{1,0:T(8,128)(2,1)} %collective-permute-done.8.refs_3_), slice={[0:24], [0:12288]} | slice | bytes 1179648 | tf_op jit(solution)/shard_map/slice | solution.py:183
  113.7 0.0 collective-permute-start.9
  113.8 0.0 copy-done.5
  113.8 0.1 select_subtract_fusion.1
  113.8 0.1 sub.59
  113.9 0.1 sub.62
  114.0 0.6 slice.36.base_ref
  114.6 0.6 fusion.8.goes_ref
  115.2 0.0 copy-done.6
  115.2 15.1 %early_product.1.refs_4_ = f32[768,512]{1,0:T(8,128)} custom-call(s32[768]{0:T(1024)} %fusion.8.goes_ref, s32[12]{0:T(128)} %bitcast.15, bf16[512,12288]{1,0:T(8,128)(2,1)} %compare_select_fusion.panel_ref, bf16[144,12288]{1,0:T(8,128)(2,1)} %copy-done.2, bf16[48,12288]{1,0:T(8,128)(2,1)} %constant_dynamic-update-slice_fusion.3.refs_1_, ...), custom_call_target="tpu_custom_call" | custom-call | tf_op jit(solution)/shard_map/early_product/pallas_call | solution.py:137
  130.3 1.6 collective-permute-done.11.refs_3_
  131.9 0.2 collective-permute-done.9.refs_2_
  132.1 0.0 collective-permute-done.3.refs_0_
  132.1 0.0 collective-permute-done.5.refs_1_
  132.1 1.2 copy-done.3
  133.3 11.6 %late_product.1 = (f32[384,512]{1,0:T(8,128)}, f32[384,512]{1,0:T(8,128)}) custom-call(s32[768]{0:T(1024)} %fusion.8.goes_ref, s32[4]{0:T(128)} %slice.36.base_ref, bf16[512,12288]{1,0:T(8,128)(2,1)} %compare_select_fusion.panel_ref, bf16[72,12288]{1,0:T(8,128)(2,1)} %collective-permute-done.3.refs_0_, bf16[72,12288]{1,0:T(8,128)(2,1)} %copy-done.3, ...), custom_call_target="tpu_custom_call" | custom-call | tf_op jit(solution)/shard_map/late_product/pallas_call | solution.py:156
  144.9 0.0 collective-permute-start.12
  144.9 2.5 %collective-permute-done.12 = f32[384,512]{1,0:T(8,128)S(1)} collective-permute-done((f32[384,512]{1,0:T(8,128)}, f32[384,512]{1,0:T(8,128)S(1)}, u32[]{:S(2)}, u32[]{:S(2)}) %collective-permute-start.12) | collective-permute-done | bytes 786464 | tf_op jit(solution)/shard_map/ppermute | solution.py:55
  147.4 1.3 add.93
  148.7 0.6 collective-permute-start.13
  149.4 2.7 %collective-permute-start.14 = (f32[96,512]{1,0:T(8,128)S(1)}, f32[96,512]{1,0:T(8,128)S(1)}, u32[]{:S(2)}, u32[]{:S(2)}) collective-permute-start(f32[96,512]{1,0:T(8,128)S(1)} %get-tuple-element.15), channel_id=1, source_target_pairs={{0,6},{1,7},{2,0},{3,1},{4,2},{5,3},{6,4},{7,5},{8,14},{9,15},{10,... | collective-permute-start | bytes 589832 | tf_op jit(solution)/shard_map/ppermute | solution.py:49
  152.1 0.0 collective-permute-start.15
  152.1 9.1 %collective-permute-done.13 = f32[96,512]{1,0:T(8,128)S(1)} collective-permute-done((f32[96,512]{1,0:T(8,128)S(1)}, f32[96,512]{1,0:T(8,128)S(1)}, u32[]{:S(2)}, u32[]{:S(2)}) %collective-permute-start.13) | collective-permute-done | bytes 196640 | tf_op jit(solution)/shard_map/ppermute | solution.py:49
  161.2 0.0 collective-permute-done.14
  161.2 0.0 collective-permute-done.15
  161.2 0.7 fusion.2
  (18 shorter events, 0.2 us)
Async XLA Ops:
  0.0 4.6 %copy-start.7 = (s32[8]{0:T(128)S(1)}, s32[8]{0:T(128)}, u32[]{:S(2)}) copy-start(s32[8]{0:T(128)} %param.10) | copy-start | bytes 100
  0.0 4.8 %copy-start.8 = (s32[8]{0:T(128)S(1)}, s32[8]{0:T(128)}, u32[]{:S(2)}) copy-start(s32[8]{0:T(128)} %param.9) | copy-start | bytes 100
  0.0 26.2 %all-to-all-start = ((bf16[6,8,12288]{2,0,1:T(8,128)(2,1)}), bf16[6,8,12288]{2,0,1:T(8,128)(2,1)S(1)}, u32[]{:S(2)}, u32[]{:S(2)}) async-start(bf16[6,8,12288]{2,0,1:T(8,128)(2,1)} %bitcast.14), calls=%async_computation | async-start | bytes 3145728 | tf_op jit(solution)/shard_map/all_to_all | solution.py:198
  26.8 16.3 %collective-permute-start = (bf16[48,12288]{1,0:T(8,128)(2,1)S(1)}, bf16[48,12288]{1,0:T(8,128)(2,1)S(1)}, u32[]{:S(2)}, u32[]{:S(2)}) collective-permute-start(bf16[48,12288]{1,0:T(8,128)(2,1)S(1)} %bitcast.11), channel_id=1, source_target_pairs={{0,32},{1,9},{2,34},{3,11},{4,36},{5,13},{6,38},{7,15},{8,40},{9,1... | collective-permute-start | bytes 3538952 | tf_op jit(solution)/shard_map/ppermute | solution.py:39
  27.4 17.4 %collective-permute-start.1 = (bf16[48,12288]{1,0:T(8,128)(2,1)S(1)}, bf16[48,12288]{1,0:T(8,128)(2,1)S(1)}, u32[]{:S(2)}, u32[]{:S(2)}) collective-permute-start(bf16[48,12288]{1,0:T(8,128)(2,1)S(1)} %bitcast.12), channel_id=1, source_target_pairs={{0,96},{1,25},{2,98},{3,27},{4,100},{5,29},{6,102},{7,31},{8,104},... | collective-permute-start | bytes 3538952 | tf_op jit(solution)/shard_map/ppermute | solution.py:39
  44.9 51.6 %copy-start.2 = (bf16[144,12288]{1,0:T(8,128)(2,1)}, bf16[144,12288]{1,0:T(8,128)(2,1)S(1)}, u32[]{:S(2)}) copy-start(bf16[144,12288]{1,0:T(8,128)(2,1)S(1)} %constant_dynamic-update-slice_fusion.refs_0_) | copy-start | bytes 10616836
  44.9 49.2 %collective-permute-start.2 = (bf16[144,12288]{1,0:T(8,128)(2,1)S(1)}, bf16[144,12288]{1,0:T(8,128)(2,1)S(1)}, u32[]{:S(2)}, u32[]{:S(2)}) collective-permute-start(bf16[144,12288]{1,0:T(8,128)(2,1)S(1)} %constant_dynamic-update-slice_fusion.refs_0_), channel_id=1, source_target_pairs={{0,8},{1,33},{2,10},{3,35},{4,12},{5,37},{6,14},{7,39},{8,16},{9,4... | collective-permute-start | bytes 10616840 | tf_op jit(solution)/shard_map/ppermute | solution.py:45
  46.9 49.5 %collective-permute-start.4 = (bf16[144,12288]{1,0:T(8,128)(2,1)S(1)}, bf16[144,12288]{1,0:T(8,128)(2,1)S(1)}, u32[]{:S(2)}, u32[]{:S(2)}) collective-permute-start(bf16[144,12288]{1,0:T(8,128)(2,1)S(1)} %constant_dynamic-update-slice_fusion.refs_0_), channel_id=1, source_target_pairs={{0,24},{1,97},{2,26},{3,99},{4,28},{5,101},{6,30},{7,103},{8,0},{9... | collective-permute-start | bytes 10616840 | tf_op jit(solution)/shard_map/ppermute | solution.py:45
  49.1 16.3 %collective-permute-start.6 = (bf16[24,12288]{1,0:T(8,128)(2,1)S(1)}, bf16[24,12288]{1,0:T(8,128)(2,1)S(1)}, u32[]{:S(2)}, u32[]{:S(2)}) collective-permute-start(bf16[24,12288]{1,0:T(8,128)(2,1)S(1)} %slice.50), channel_id=1, source_target_pairs={{0,32},{1,9},{2,34},{3,11},{4,36},{5,13},{6,38},{7,15},{8,40},{9,1... | collective-permute-start | bytes 1769480 | tf_op jit(solution)/shard_map/ppermute | solution.py:39
  49.5 17.5 %collective-permute-start.7 = (bf16[24,12288]{1,0:T(8,128)(2,1)S(1)}, bf16[24,12288]{1,0:T(8,128)(2,1)S(1)}, u32[]{:S(2)}, u32[]{:S(2)}) collective-permute-start(bf16[24,12288]{1,0:T(8,128)(2,1)S(1)} %slice.51), channel_id=1, source_target_pairs={{0,96},{1,25},{2,98},{3,27},{4,100},{5,29},{6,102},{7,31},{8,104},... | collective-permute-start | bytes 1769480 | tf_op jit(solution)/shard_map/ppermute | solution.py:39
  67.9 38.7 %collective-permute-start.10 = (bf16[48,12288]{1,0:T(8,128)(2,1)}, bf16[48,12288]{1,0:T(8,128)(2,1)}, u32[]{:S(2)}, u32[]{:S(2)}) collective-permute-start(bf16[48,12288]{1,0:T(8,128)(2,1)} %constant_dynamic-update-slice_fusion.3.refs_1_), channel_id=1, source_target_pairs={{0,24},{1,97},{2,26},{3,99},{4,28},{5,101},{6,30},{7,103},{8,0},{9... | collective-permute-start | bytes 3538952 | tf_op jit(solution)/shard_map/ppermute | solution.py:45
  69.9 41.9 %collective-permute-start.8 = (bf16[48,12288]{1,0:T(8,128)(2,1)}, bf16[48,12288]{1,0:T(8,128)(2,1)}, u32[]{:S(2)}, u32[]{:S(2)}) collective-permute-start(bf16[48,12288]{1,0:T(8,128)(2,1)} %constant_dynamic-update-slice_fusion.3.refs_1_), channel_id=1, source_target_pairs={{0,8},{1,33},{2,10},{3,35},{4,12},{5,37},{6,14},{7,39},{8,16},{9,4... | collective-permute-start | bytes 3538952 | tf_op jit(solution)/shard_map/ppermute | solution.py:45
  94.1 2.3 %copy-start = (bf16[144,12288]{1,0:T(8,128)(2,1)}, bf16[144,12288]{1,0:T(8,128)(2,1)S(1)}, u32[]{:S(2)}) copy-start(bf16[144,12288]{1,0:T(8,128)(2,1)S(1)} %collective-permute-done.2.refs_2_) | copy-start | bytes 10616836
  96.4 35.7 %collective-permute-start.3 = (bf16[72,12288]{1,0:T(8,128)(2,1)}, bf16[72,12288]{1,0:T(8,128)(2,1)}, u32[]{:S(2)}, u32[]{:S(2)}) collective-permute-start(bf16[72,12288]{1,0:T(8,128)(2,1)} %slice.48), channel_id=1, source_target_pairs={{0,8},{1,33},{2,10},{3,35},{4,12},{5,37},{6,14},{7,39},{8,16},{9,4... | collective-permute-start | bytes 5308424 | tf_op jit(solution)/shard_map/ppermute | solution.py:45
  96.4 1.8 %copy-start.1 = (bf16[144,12288]{1,0:T(8,128)(2,1)}, bf16[144,12288]{1,0:T(8,128)(2,1)S(1)}, u32[]{:S(2)}) copy-start(bf16[144,12288]{1,0:T(8,128)(2,1)S(1)} %collective-permute-done.4.refs_4_) | copy-start | bytes 10616836
  98.2 15.6 %copy-start.5 = (s32[4]{0:T(128)S(1)}, s32[4]{0:T(128)}, u32[]{:S(2)}) copy-start(s32[4]{0:T(128)} %constant.116.clone) | copy-start | bytes 52
  98.2 16.4 %copy-start.4 = (s32[768]{0:T(1024)S(1)}, s32[768]{0:T(1024)}, u32[]{:S(2)}) copy-start(s32[768]{0:T(1024)} %param.11) | copy-start | bytes 9220
  98.2 33.9 %collective-permute-start.5 = (bf16[72,12288]{1,0:T(8,128)(2,1)S(1)}, bf16[72,12288]{1,0:T(8,128)(2,1)S(1)}, u32[]{:S(2)}, u32[]{:S(2)}) collective-permute-start(bf16[72,12288]{1,0:T(8,128)(2,1)S(1)} %slice.49), channel_id=1, source_target_pairs={{0,24},{1,97},{2,26},{3,99},{4,28},{5,101},{6,30},{7,103},{8,0},{9... | collective-permute-start | bytes 5308424 | tf_op jit(solution)/shard_map/ppermute | solution.py:45
  108.5 23.3 %collective-permute-start.11 = (bf16[24,12288]{1,0:T(8,128)(2,1)}, bf16[24,12288]{1,0:T(8,128)(2,1)}, u32[]{:S(2)}, u32[]{:S(2)}) collective-permute-start(bf16[24,12288]{1,0:T(8,128)(2,1)} %slice.53), channel_id=1, source_target_pairs={{0,24},{1,97},{2,26},{3,99},{4,28},{5,101},{6,30},{7,103},{8,0},{9... | collective-permute-start | bytes 1769480 | tf_op jit(solution)/shard_map/ppermute | solution.py:45
  113.7 18.4 %collective-permute-start.9 = (bf16[24,12288]{1,0:T(8,128)(2,1)}, bf16[24,12288]{1,0:T(8,128)(2,1)}, u32[]{:S(2)}, u32[]{:S(2)}) collective-permute-start(bf16[24,12288]{1,0:T(8,128)(2,1)} %slice.52), channel_id=1, source_target_pairs={{0,8},{1,33},{2,10},{3,35},{4,12},{5,37},{6,14},{7,39},{8,16},{9,4... | collective-permute-start | bytes 1769480 | tf_op jit(solution)/shard_map/ppermute | solution.py:45
  114.0 1.2 copy-start.6
  132.1 1.2 copy-start.3
  144.9 2.5 %collective-permute-start.12 = (f32[384,512]{1,0:T(8,128)}, f32[384,512]{1,0:T(8,128)S(1)}, u32[]{:S(2)}, u32[]{:S(2)}) collective-permute-start(f32[384,512]{1,0:T(8,128)} %get-tuple-element.12), channel_id=1, source_target_pairs={{0,1},{1,0},{2,3},{3,2},{4,5},{5,4},{6,7},{7,6},{8,9},{9,8},{10,11... | collective-permute-start | bytes 2359304 | tf_op jit(solution)/shard_map/ppermute | solution.py:55
  148.7 12.4 %collective-permute-start.13 = (f32[96,512]{1,0:T(8,128)S(1)}, f32[96,512]{1,0:T(8,128)S(1)}, u32[]{:S(2)}, u32[]{:S(2)}) collective-permute-start(f32[96,512]{1,0:T(8,128)S(1)} %get-tuple-element.13), channel_id=1, source_target_pairs={{0,2},{1,3},{2,4},{3,5},{4,6},{5,7},{6,0},{7,1},{8,10},{9,11},{10,... | collective-permute-start | bytes 589832 | tf_op jit(solution)/shard_map/ppermute | solution.py:49
  149.4 11.8 %collective-permute-start.14 = (f32[96,512]{1,0:T(8,128)S(1)}, f32[96,512]{1,0:T(8,128)S(1)}, u32[]{:S(2)}, u32[]{:S(2)}) collective-permute-start(f32[96,512]{1,0:T(8,128)S(1)} %get-tuple-element.15), channel_id=1, source_target_pairs={{0,6},{1,7},{2,0},{3,1},{4,2},{5,3},{6,4},{7,5},{8,14},{9,15},{10,... | collective-permute-start | bytes 589832 | tf_op jit(solution)/shard_map/ppermute | solution.py:49
  152.1 9.1 %collective-permute-start.15 = (f32[96,512]{1,0:T(8,128)S(1)}, f32[96,512]{1,0:T(8,128)S(1)}, u32[]{:S(2)}, u32[]{:S(2)}) collective-permute-start(f32[96,512]{1,0:T(8,128)S(1)} %get-tuple-element.14), channel_id=1, source_target_pairs={{0,4},{1,5},{2,6},{3,7},{4,0},{5,1},{6,2},{7,3},{8,12},{9,13},{10,... | collective-permute-start | bytes 589832 | tf_op jit(solution)/shard_map/ppermute | solution.py:49

commit v3 on v2

--- a/solution.py
+++ b/solution.py
@@ -103,23 +103,29 @@
 
 
 def late_kernel(per_device, goes_ref, base_ref, panel_ref, *refs):
-    *piece_refs, early_ref, mine_ref, theirs_ref, total_ref, all_ref, joined_ref = refs
+    *piece_refs, early_ref, mine_ref, theirs_ref, total_ref, all_ref, joined_ref, sems = refs
     step = pl.program_id(0)
+    half = mine_ref.shape[0]
+    placed_before = pltpu.make_async_copy(early_ref, all_ref, sems.at[0])
 
     @pl.when(step == 0)
     def _():
+        placed_before.start()
         total_ref[...] = jnp.zeros_like(total_ref)
-        all_ref[...] = early_ref[...]
 
     join(piece_refs, joined_ref)
     total_ref[...] += product(joined_ref[...], panel_ref[...])
 
     @pl.when(step == pl.num_programs(0) - 1)
     def _():
+        placed_before.wait()
         place_rows(goes_ref, base_ref, total_ref, all_ref, SIDE, per_device)
-        half = mine_ref.shape[0]
-        mine_ref[...] = all_ref[pl.ds(0, half), :]
-        theirs_ref[...] = all_ref[pl.ds(half, half), :]
+        out = [pltpu.make_async_copy(all_ref.at[pl.ds(at * half, half), :], ref, sems.at[1 + at])
+               for at, ref in enumerate((mine_ref, theirs_ref))]
+        for copy in out:
+            copy.start()
+        for copy in out:
+            copy.wait()
 
 
 def by_step(height):
@@ -145,6 +151,7 @@
             scratch_shapes=[pltpu.VMEM((count, rows), jnp.float32),
                             pltpu.VMEM((count, BLOCK), panel.dtype)],
         ),
+        compiler_params=pltpu.CompilerParams(vmem_limit_bytes=28 << 20),
         name="early_product",
     )(goes, bases, panel, *pieces)
 
@@ -160,12 +167,14 @@
             num_scalar_prefetch=2,
             grid=(depth // BLOCK,),
             in_specs=[by_step(value.shape[0]) for value in (panel, *pieces)]
-            + [at_once(pairs, rows)],
-            out_specs=[at_once(pairs // 2, rows)] * 2,
+            + [pl.BlockSpec(memory_space=pltpu.HBM)],
+            out_specs=[pl.BlockSpec(memory_space=pltpu.HBM)] * 2,
             scratch_shapes=[pltpu.VMEM((count, rows), jnp.float32),
                             pltpu.VMEM((pairs, rows), jnp.float32),
-                            pltpu.VMEM((count, BLOCK), panel.dtype)],
+                            pltpu.VMEM((count, BLOCK), panel.dtype),
+                            pltpu.SemaphoreType.DMA((3,))],
         ),
+        compiler_params=pltpu.CompilerParams(vmem_limit_bytes=18 << 20),
         name="late_product",
     )(goes, bases, panel, *pieces, early)
 

time: 163 us -> 157 us (0.963)
  Pallas kernels: 26.7 us -> 20.8 us
  local copies, waits for them, and re-layouts: 12.6 us -> 16.6 us
  waiting for transfers between devices: 82.6 us -> 80.7 us
  other arithmetic: 15 us -> 13.2 us
    pallas_call x1, Pallas kernels: 11.6 us -> 7.97 us  [late_product(): pl.pallas_call(functools.partial(late_kernel, per_device), out_shape=[jax...]
    unnamed x21 -> x25, local copies, waits for them, and re-layouts: 4.7 us -> 7.93 us
    pallas_call x1, Pallas kernels: 15.1 us -> 12.8 us  [early_product(): pl.pallas_call(functools.partial(early_kernel, per_device), out_shape=jax...]
    ppermute x8, waiting for transfers between devices: 31.1 us -> 29.4 us  [along_second(): return lax.ppermute(value, ('row', 'col'), device_pairs(move))]
  transfers between devices with their start and end apart: 17 -> 17, of which waited for: 11 -> 11; matrix products, arithmetic and copies ran while one was open for 13% -> 14% of each run, Pallas kernels for 9% -> 8%
where the time goes in v3:
time: 157 us
  waiting for transfers between devices  80.7 us (51%)
  starting transfers between devices  25.1 us (16%)
  Pallas kernels  20.8 us (13%)
  local copies, waits for them, and re-layouts  16.6 us (11%)
  other arithmetic  13.2 us (8%)
    ppermute x4, waiting for transfers between devices, along_first(): return lax.ppermute(value, ('row', 'col'), device_pairs(move))  30.6 us
    ppermute x8, waiting for transfers between devices, along_second(): return lax.ppermute(value, ('row', 'col'), device_pairs(move))  29.4 us
    ppermute x8, starting transfers between devices, along_second(): return lax.ppermute(value, ('row', 'col'), device_pairs(move))  12.9 us
    pallas_call x1, Pallas kernels, early_product(): pl.pallas_call(functools.partial(early_kernel, per_device), out_shape=jax...  12.8 us
    select_n x1, other arithmetic, on_device(): jnp.where(row_irrep[:, None] == col_irrep[None, :], hole_panel, jnp.zeros...  11.6 us
    all_to_all x1, waiting for transfers between devices, on_device(): own = lax.all_to_all(split, 'col', split_axis=1, concat_axis=1, tiled=True)  9.34 us
    ppermute x3, waiting for transfers between devices, along_y(): lax.ppermute(value, ('row', 'col'), device_pairs(lambda x, z, y, core: (x...  9.13 us
    pallas_call x1, Pallas kernels, late_product(): pl.pallas_call(functools.partial(late_kernel, per_device), out_shape=[jax...  7.97 us
  transfers between devices with their start and end apart: 17, of which 11 were waited for; matrix products, arithmetic and copies ran while one was open for 14% of the time, Pallas kernels for 8%

profile of v3, /device:TPU:6, one launch (start us, length us, event | category | flops | bytes accessed | tf_op | source)
XLA Modules:
  0.0 156.6 jit_solution(5868682380019396868)
XLA Ops:
  0.0 4.6 %all-to-all-start = ((bf16[6,8,12288]{2,0,1:T(8,128)(2,1)}), bf16[6,8,12288]{2,0,1:T(8,128)(2,1)S(1)}, u32[]{:S(2)}, u32[]{:S(2)}) async-start(bf16[6,8,12288]{2,0,1:T(8,128)(2,1)} %bitcast.17), calls=%async_computation | async-start | bytes 3145728 | tf_op jit(solution)/shard_map/all_to_all | solution.py:207
  4.6 0.2 reduce-window.17
  4.8 0.2 reduce-window.16
  5.0 0.2 convert_reduce_fusion
  5.2 0.1 convert_reduce_fusion.1
  5.3 11.6 %compare_select_fusion.panel_ref = bf16[512,12288]{1,0:T(8,128)(2,1)} fusion(bf16[512,12288]{1,0:T(8,128)(2,1)} %param.7, s32[12288]{0:T(1024)S(1)} %convert_reduce_fusion, s32[512]{0:T(512)S(1)} %convert_reduce_fusion.1), kind=kLoop, calls=%fused_computation | loop fusion | flops 12582912 | bytes 25217024 | tf_op jit(solution)/shard_map/jit(_where)/select_n | solution.py:212
  16.9 9.3 %all-to-all-done = bf16[6,8,12288]{2,0,1:T(8,128)(2,1)S(1)} async-done(((bf16[6,8,12288]{2,0,1:T(8,128)(2,1)}), bf16[6,8,12288]{2,0,1:T(8,128)(2,1)S(1)}, u32[]{:S(2)}, u32[]{:S(2)}) %all-to-all-start) | async-done | bytes 1179680 | tf_op jit(solution)/shard_map/all_to_all | solution.py:207
  26.2 0.7 copy.11
  26.8 0.5 collective-permute-start
  27.4 1.5 collective-permute-start.1
  28.9 0.1 constant_dynamic-update-slice_fusion.2
  29.0 14.1 %collective-permute-done = bf16[48,12288]{1,0:T(8,128)(2,1)S(1)} collective-permute-done((bf16[48,12288]{1,0:T(8,128)(2,1)S(1)}, bf16[48,12288]{1,0:T(8,128)(2,1)S(1)}, u32[]{:S(2)}, u32[]{:S(2)}) %collective-permute-start) | collective-permute-done | bytes 1179680 | tf_op jit(solution)/shard_map/ppermute | solution.py:39
  43.1 0.1 constant_dynamic-update-slice_fusion.1
  43.2 1.6 %collective-permute-done.1 = bf16[48,12288]{1,0:T(8,128)(2,1)S(1)} collective-permute-done((bf16[48,12288]{1,0:T(8,128)(2,1)S(1)}, bf16[48,12288]{1,0:T(8,128)(2,1)S(1)}, u32[]{:S(2)}, u32[]{:S(2)}) %collective-permute-start.1) | collective-permute-done | bytes 1179680 | tf_op jit(solution)/shard_map/ppermute | solution.py:39
  44.8 0.1 constant_dynamic-update-slice_fusion.refs_0_
  44.9 2.0 %collective-permute-start.2 = (bf16[144,12288]{1,0:T(8,128)(2,1)S(1)}, bf16[144,12288]{1,0:T(8,128)(2,1)S(1)}, u32[]{:S(2)}, u32[]{:S(2)}) collective-permute-start(bf16[144,12288]{1,0:T(8,128)(2,1)S(1)} %constant_dynamic-update-slice_fusion.refs_0_), channel_id=1, source_target_pairs={{0,8},{1,33},{2,10},{3,35},{4,12},{5,37},{6,14},{7,39},{8,16},{9,4... | collective-permute-start | bytes 10616840 | tf_op jit(solution)/shard_map/ppermute | solution.py:45
  46.9 2.2 %collective-permute-start.4 = (bf16[144,12288]{1,0:T(8,128)(2,1)S(1)}, bf16[144,12288]{1,0:T(8,128)(2,1)S(1)}, u32[]{:S(2)}, u32[]{:S(2)}) collective-permute-start(bf16[144,12288]{1,0:T(8,128)(2,1)S(1)} %constant_dynamic-update-slice_fusion.refs_0_), channel_id=1, source_target_pairs={{0,24},{1,97},{2,26},{3,99},{4,28},{5,101},{6,30},{7,103},{8,0},{9... | collective-permute-start | bytes 10616840 | tf_op jit(solution)/shard_map/ppermute | solution.py:45
  49.1 1.7 %copy-done.2 = bf16[144,12288]{1,0:T(8,128)(2,1)} copy-done((bf16[144,12288]{1,0:T(8,128)(2,1)}, bf16[144,12288]{1,0:T(8,128)(2,1)S(1)}, u32[]{:S(2)}) %copy-start.2) | copy-done | bytes 3538968
  50.9 0.3 collective-permute-start.6
  51.3 1.8 %collective-permute-start.7 = (bf16[24,12288]{1,0:T(8,128)(2,1)S(1)}, bf16[24,12288]{1,0:T(8,128)(2,1)S(1)}, u32[]{:S(2)}, u32[]{:S(2)}) collective-permute-start(bf16[24,12288]{1,0:T(8,128)(2,1)S(1)} %slice.51), channel_id=1, source_target_pairs={{0,96},{1,25},{2,98},{3,27},{4,100},{5,29},{6,102},{7,31},{8,104},... | collective-permute-start | bytes 1769480 | tf_op jit(solution)/shard_map/ppermute | solution.py:39
  53.1 14.1 %collective-permute-done.6 = bf16[24,12288]{1,0:T(8,128)(2,1)S(1)} collective-permute-done((bf16[24,12288]{1,0:T(8,128)(2,1)S(1)}, bf16[24,12288]{1,0:T(8,128)(2,1)S(1)}, u32[]{:S(2)}, u32[]{:S(2)}) %collective-permute-start.6) | collective-permute-done | bytes 589856 | tf_op jit(solution)/shard_map/ppermute | solution.py:39
  67.2 0.9 constant_dynamic-update-slice_fusion.4
  68.1 0.7 collective-permute-done.7
  68.8 0.9 constant_dynamic-update-slice_fusion.3.refs_1_
  69.7 1.9 %collective-permute-start.10 = (bf16[48,12288]{1,0:T(8,128)(2,1)}, bf16[48,12288]{1,0:T(8,128)(2,1)}, u32[]{:S(2)}, u32[]{:S(2)}) collective-permute-start(bf16[48,12288]{1,0:T(8,128)(2,1)} %constant_dynamic-update-slice_fusion.3.refs_1_), channel_id=1, source_target_pairs={{0,24},{1,97},{2,26},{3,99},{4,28},{5,101},{6,30},{7,103},{8,0},{9... | collective-permute-start | bytes 3538952 | tf_op jit(solution)/shard_map/ppermute | solution.py:45
  71.6 0.1 collective-permute-start.8
  71.7 23.1 %collective-permute-done.2.refs_2_ = bf16[144,12288]{1,0:T(8,128)(2,1)S(1)} collective-permute-done((bf16[144,12288]{1,0:T(8,128)(2,1)S(1)}, bf16[144,12288]{1,0:T(8,128)(2,1)S(1)}, u32[]{:S(2)}, u32[]{:S(2)}) %collective-permute-start.2) | collective-permute-done | bytes 3538976 | tf_op jit(solution)/shard_map/ppermute | solution.py:45
  94.8 1.4 slice.48
  96.2 0.0 collective-permute-start.3
  96.2 0.0 collective-permute-done.4.refs_4_
  96.2 1.5 slice.49
  97.7 0.8 copy-done
  98.5 3.2 %collective-permute-start.5 = (bf16[72,12288]{1,0:T(8,128)(2,1)}, bf16[72,12288]{1,0:T(8,128)(2,1)}, u32[]{:S(2)}, u32[]{:S(2)}) collective-permute-start(bf16[72,12288]{1,0:T(8,128)(2,1)} %slice.49), channel_id=1, source_target_pairs={{0,24},{1,97},{2,26},{3,99},{4,28},{5,101},{6,30},{7,103},{8,0},{9... | collective-permute-start | bytes 5308424 | tf_op jit(solution)/shard_map/ppermute | solution.py:45
  101.7 5.7 %collective-permute-done.10.refs_5_ = bf16[48,12288]{1,0:T(8,128)(2,1)} collective-permute-done((bf16[48,12288]{1,0:T(8,128)(2,1)}, bf16[48,12288]{1,0:T(8,128)(2,1)}, u32[]{:S(2)}, u32[]{:S(2)}) %collective-permute-start.10) | collective-permute-done | bytes 1179680 | tf_op jit(solution)/shard_map/ppermute | solution.py:45
  107.4 1.9 %slice.53 = bf16[24,12288]{1,0:T(8,128)(2,1)} slice(bf16[48,12288]{1,0:T(8,128)(2,1)} %collective-permute-done.10.refs_5_), slice={[24:48], [0:12288]} | slice | bytes 1179648 | tf_op jit(solution)/shard_map/slice | solution.py:192
  109.3 3.4 %collective-permute-start.11 = (bf16[24,12288]{1,0:T(8,128)(2,1)}, bf16[24,12288]{1,0:T(8,128)(2,1)}, u32[]{:S(2)}, u32[]{:S(2)}) collective-permute-start(bf16[24,12288]{1,0:T(8,128)(2,1)} %slice.53), channel_id=1, source_target_pairs={{0,24},{1,97},{2,26},{3,99},{4,28},{5,101},{6,30},{7,103},{8,0},{9... | collective-permute-start | bytes 1769480 | tf_op jit(solution)/shard_map/ppermute | solution.py:45
  112.8 0.0 collective-permute-done.8.refs_3_
  112.8 1.9 %slice.52 = bf16[24,12288]{1,0:T(8,128)(2,1)} slice(bf16[48,12288]{1,0:T(8,128)(2,1)} %collective-permute-done.8.refs_3_), slice={[0:24], [0:12288]} | slice | bytes 1179648 | tf_op jit(solution)/shard_map/slice | solution.py:192
  114.7 0.0 collective-permute-start.9
  114.7 0.1 select_subtract_fusion.1
  114.8 0.1 sub.59
  114.8 0.1 sub.62
  114.9 0.1 slice.36.base_ref
  115.0 0.0 slice-start
  115.1 0.0 copy-start.1
  115.1 2.1 %copy-done.1 = bf16[144,12288]{1,0:T(8,128)(2,1)S(1)} copy-done((bf16[144,12288]{1,0:T(8,128)(2,1)S(1)}, bf16[144,12288]{1,0:T(8,128)(2,1)}, u32[]{:S(2)}) %copy-start.1) | copy-done | bytes 3538968
  117.2 2.2 %copy-done.3 = bf16[144,12288]{1,0:T(8,128)(2,1)S(1)} copy-done((bf16[144,12288]{1,0:T(8,128)(2,1)S(1)}, bf16[144,12288]{1,0:T(8,128)(2,1)}, u32[]{:S(2)}) %copy-start.3) | copy-done | bytes 3538968
  119.4 12.8 %early_product.1.refs_4_ = f32[768,512]{1,0:T(8,128)S(1)} custom-call(s32[768]{0:T(1024)S(1)} %fusion.8.goes_ref, s32[12]{0:T(128)S(1)} %bitcast.13, bf16[512,12288]{1,0:T(8,128)(2,1)} %compare_select_fusion.panel_ref, bf16[144,12288]{1,0:T(8,128)(2,1)S(1)} %copy-done.3, bf16[48,12288]{1,0:T(8,128)(2,1)} %constant_dynamic-update-slice_fusion.3.refs_1_, ...), custom_call_target="tpu_custom_call" | custom-call | tf_op jit(solution)/shard_map/early_product/pallas_call | solution.py:143
  132.2 0.5 collective-permute-done.11.refs_3_
  132.7 0.1 collective-permute-done.9.refs_2_
  132.8 0.0 collective-permute-done.3.refs_0_
  132.8 0.0 collective-permute-done.5.refs_1_
  132.8 0.0 slice-done
  132.8 8.0 %late_product.1 = (f32[384,512]{1,0:T(8,128)S(1)}, f32[384,512]{1,0:T(8,128)S(1)}) custom-call(s32[768]{0:T(1024)S(1)} %fusion.8.goes_ref, s32[4]{0:T(128)S(1)} %slice.36.base_ref, bf16[512,12288]{1,0:T(8,128)(2,1)S(1)} %bitcast.12, bf16[72,12288]{1,0:T(8,128)(2,1)} %collective-permute-done.3.refs_0_, bf16[72,12288]{1,0:T(8,128)(2,1)} %collective-permute-done.5.refs_1_, ...), custom_call_target="tpu_custom_call" | custom-call | tf_op jit(solution)/shard_map/late_product/pallas_call | solution.py:163
  140.8 0.1 collective-permute-start.12
  140.9 2.3 %collective-permute-done.12 = f32[384,512]{1,0:T(8,128)S(1)} collective-permute-done((f32[384,512]{1,0:T(8,128)S(1)}, f32[384,512]{1,0:T(8,128)S(1)}, u32[]{:S(2)}, u32[]{:S(2)}) %collective-permute-start.12) | collective-permute-done | bytes 786464 | tf_op jit(solution)/shard_map/ppermute | solution.py:55
  143.2 0.1 add.93
  143.4 0.6 collective-permute-start.13
  144.0 2.7 %collective-permute-start.14 = (f32[96,512]{1,0:T(8,128)S(1)}, f32[96,512]{1,0:T(8,128)S(1)}, u32[]{:S(2)}, u32[]{:S(2)}) collective-permute-start(f32[96,512]{1,0:T(8,128)S(1)} %get-tuple-element.15), channel_id=1, source_target_pairs={{0,6},{1,7},{2,0},{3,1},{4,2},{5,3},{6,4},{7,5},{8,14},{9,15},{10,... | collective-permute-start | bytes 589832 | tf_op jit(solution)/shard_map/ppermute | solution.py:49
  146.7 0.0 collective-permute-start.15
  146.7 9.1 %collective-permute-done.13 = f32[96,512]{1,0:T(8,128)S(1)} collective-permute-done((f32[96,512]{1,0:T(8,128)S(1)}, f32[96,512]{1,0:T(8,128)S(1)}, u32[]{:S(2)}, u32[]{:S(2)}) %collective-permute-start.13) | collective-permute-done | bytes 196640 | tf_op jit(solution)/shard_map/ppermute | solution.py:49
  155.8 0.0 collective-permute-done.14
  155.8 0.0 collective-permute-done.15
  155.8 0.7 fusion.2
  (23 shorter events, 0.2 us)
Async XLA Ops:
  0.0 4.6 %copy-start.6 = (s32[8]{0:T(128)S(1)}, s32[8]{0:T(128)}, u32[]{:S(2)}) copy-start(s32[8]{0:T(128)} %param.10) | copy-start | bytes 100
  0.0 4.8 %copy-start.7 = (s32[8]{0:T(128)S(1)}, s32[8]{0:T(128)}, u32[]{:S(2)}) copy-start(s32[8]{0:T(128)} %param.9) | copy-start | bytes 100
  0.0 26.2 %all-to-all-start = ((bf16[6,8,12288]{2,0,1:T(8,128)(2,1)}), bf16[6,8,12288]{2,0,1:T(8,128)(2,1)S(1)}, u32[]{:S(2)}, u32[]{:S(2)}) async-start(bf16[6,8,12288]{2,0,1:T(8,128)(2,1)} %bitcast.17), calls=%async_computation | async-start | bytes 3145728 | tf_op jit(solution)/shard_map/all_to_all | solution.py:207
  26.8 16.3 %collective-permute-start = (bf16[48,12288]{1,0:T(8,128)(2,1)S(1)}, bf16[48,12288]{1,0:T(8,128)(2,1)S(1)}, u32[]{:S(2)}, u32[]{:S(2)}) collective-permute-start(bf16[48,12288]{1,0:T(8,128)(2,1)S(1)} %bitcast.14), channel_id=1, source_target_pairs={{0,32},{1,9},{2,34},{3,11},{4,36},{5,13},{6,38},{7,15},{8,40},{9,1... | collective-permute-start | bytes 3538952 | tf_op jit(solution)/shard_map/ppermute | solution.py:39
  27.4 17.4 %collective-permute-start.1 = (bf16[48,12288]{1,0:T(8,128)(2,1)S(1)}, bf16[48,12288]{1,0:T(8,128)(2,1)S(1)}, u32[]{:S(2)}, u32[]{:S(2)}) collective-permute-start(bf16[48,12288]{1,0:T(8,128)(2,1)S(1)} %bitcast.15), channel_id=1, source_target_pairs={{0,96},{1,25},{2,98},{3,27},{4,100},{5,29},{6,102},{7,31},{8,104},... | collective-permute-start | bytes 3538952 | tf_op jit(solution)/shard_map/ppermute | solution.py:39
  44.9 49.9 %collective-permute-start.2 = (bf16[144,12288]{1,0:T(8,128)(2,1)S(1)}, bf16[144,12288]{1,0:T(8,128)(2,1)S(1)}, u32[]{:S(2)}, u32[]{:S(2)}) collective-permute-start(bf16[144,12288]{1,0:T(8,128)(2,1)S(1)} %constant_dynamic-update-slice_fusion.refs_0_), channel_id=1, source_target_pairs={{0,8},{1,33},{2,10},{3,35},{4,12},{5,37},{6,14},{7,39},{8,16},{9,4... | collective-permute-start | bytes 10616840 | tf_op jit(solution)/shard_map/ppermute | solution.py:45
  46.9 49.3 %collective-permute-start.4 = (bf16[144,12288]{1,0:T(8,128)(2,1)S(1)}, bf16[144,12288]{1,0:T(8,128)(2,1)S(1)}, u32[]{:S(2)}, u32[]{:S(2)}) collective-permute-start(bf16[144,12288]{1,0:T(8,128)(2,1)S(1)} %constant_dynamic-update-slice_fusion.refs_0_), channel_id=1, source_target_pairs={{0,24},{1,97},{2,26},{3,99},{4,28},{5,101},{6,30},{7,103},{8,0},{9... | collective-permute-start | bytes 10616840 | tf_op jit(solution)/shard_map/ppermute | solution.py:45
  49.1 1.7 %copy-start.2 = (bf16[144,12288]{1,0:T(8,128)(2,1)}, bf16[144,12288]{1,0:T(8,128)(2,1)S(1)}, u32[]{:S(2)}) copy-start(bf16[144,12288]{1,0:T(8,128)(2,1)S(1)} %constant_dynamic-update-slice_fusion.refs_0_) | copy-start | bytes 10616836
  50.9 16.3 %collective-permute-start.6 = (bf16[24,12288]{1,0:T(8,128)(2,1)S(1)}, bf16[24,12288]{1,0:T(8,128)(2,1)S(1)}, u32[]{:S(2)}, u32[]{:S(2)}) collective-permute-start(bf16[24,12288]{1,0:T(8,128)(2,1)S(1)} %slice.50), channel_id=1, source_target_pairs={{0,32},{1,9},{2,34},{3,11},{4,36},{5,13},{6,38},{7,15},{8,40},{9,1... | collective-permute-start | bytes 1769480 | tf_op jit(solution)/shard_map/ppermute | solution.py:39
  51.3 17.5 %collective-permute-start.7 = (bf16[24,12288]{1,0:T(8,128)(2,1)S(1)}, bf16[24,12288]{1,0:T(8,128)(2,1)S(1)}, u32[]{:S(2)}, u32[]{:S(2)}) collective-permute-start(bf16[24,12288]{1,0:T(8,128)(2,1)S(1)} %slice.51), channel_id=1, source_target_pairs={{0,96},{1,25},{2,98},{3,27},{4,100},{5,29},{6,102},{7,31},{8,104},... | collective-permute-start | bytes 1769480 | tf_op jit(solution)/shard_map/ppermute | solution.py:39
  69.7 37.7 %collective-permute-start.10 = (bf16[48,12288]{1,0:T(8,128)(2,1)}, bf16[48,12288]{1,0:T(8,128)(2,1)}, u32[]{:S(2)}, u32[]{:S(2)}) collective-permute-start(bf16[48,12288]{1,0:T(8,128)(2,1)} %constant_dynamic-update-slice_fusion.3.refs_1_), channel_id=1, source_target_pairs={{0,24},{1,97},{2,26},{3,99},{4,28},{5,101},{6,30},{7,103},{8,0},{9... | collective-permute-start | bytes 3538952 | tf_op jit(solution)/shard_map/ppermute | solution.py:45
  71.6 41.1 %collective-permute-start.8 = (bf16[48,12288]{1,0:T(8,128)(2,1)}, bf16[48,12288]{1,0:T(8,128)(2,1)}, u32[]{:S(2)}, u32[]{:S(2)}) collective-permute-start(bf16[48,12288]{1,0:T(8,128)(2,1)} %constant_dynamic-update-slice_fusion.3.refs_1_), channel_id=1, source_target_pairs={{0,8},{1,33},{2,10},{3,35},{4,12},{5,37},{6,14},{7,39},{8,16},{9,4... | collective-permute-start | bytes 3538952 | tf_op jit(solution)/shard_map/ppermute | solution.py:45
  96.2 36.6 %collective-permute-start.3 = (bf16[72,12288]{1,0:T(8,128)(2,1)}, bf16[72,12288]{1,0:T(8,128)(2,1)}, u32[]{:S(2)}, u32[]{:S(2)}) collective-permute-start(bf16[72,12288]{1,0:T(8,128)(2,1)} %slice.48), channel_id=1, source_target_pairs={{0,8},{1,33},{2,10},{3,35},{4,12},{5,37},{6,14},{7,39},{8,16},{9,4... | collective-permute-start | bytes 5308424 | tf_op jit(solution)/shard_map/ppermute | solution.py:45
  96.2 2.3 %copy-start = (bf16[144,12288]{1,0:T(8,128)(2,1)}, bf16[144,12288]{1,0:T(8,128)(2,1)S(1)}, u32[]{:S(2)}) copy-start(bf16[144,12288]{1,0:T(8,128)(2,1)S(1)} %collective-permute-done.4.refs_4_) | copy-start | bytes 10616836
  98.5 16.2 %copy-start.5 = (s32[4]{0:T(128)S(1)}, s32[4]{0:T(128)}, u32[]{:S(2)}) copy-start(s32[4]{0:T(128)} %constant.116.clone) | copy-start | bytes 52
  98.5 16.5 %copy-start.4 = (s32[768]{0:T(1024)S(1)}, s32[768]{0:T(1024)}, u32[]{:S(2)}) copy-start(s32[768]{0:T(1024)} %param.11) | copy-start | bytes 9220
  98.5 34.3 %collective-permute-start.5 = (bf16[72,12288]{1,0:T(8,128)(2,1)}, bf16[72,12288]{1,0:T(8,128)(2,1)}, u32[]{:S(2)}, u32[]{:S(2)}) collective-permute-start(bf16[72,12288]{1,0:T(8,128)(2,1)} %slice.49), channel_id=1, source_target_pairs={{0,24},{1,97},{2,26},{3,99},{4,28},{5,101},{6,30},{7,103},{8,0},{9... | collective-permute-start | bytes 5308424 | tf_op jit(solution)/shard_map/ppermute | solution.py:45
  109.3 23.4 %collective-permute-start.11 = (bf16[24,12288]{1,0:T(8,128)(2,1)}, bf16[24,12288]{1,0:T(8,128)(2,1)}, u32[]{:S(2)}, u32[]{:S(2)}) collective-permute-start(bf16[24,12288]{1,0:T(8,128)(2,1)} %slice.53), channel_id=1, source_target_pairs={{0,24},{1,97},{2,26},{3,99},{4,28},{5,101},{6,30},{7,103},{8,0},{9... | collective-permute-start | bytes 1769480 | tf_op jit(solution)/shard_map/ppermute | solution.py:45
  114.7 18.1 %collective-permute-start.9 = (bf16[24,12288]{1,0:T(8,128)(2,1)}, bf16[24,12288]{1,0:T(8,128)(2,1)}, u32[]{:S(2)}, u32[]{:S(2)}) collective-permute-start(bf16[24,12288]{1,0:T(8,128)(2,1)} %slice.52), channel_id=1, source_target_pairs={{0,8},{1,33},{2,10},{3,35},{4,12},{5,37},{6,14},{7,39},{8,16},{9,4... | collective-permute-start | bytes 1769480 | tf_op jit(solution)/shard_map/ppermute | solution.py:45
  115.0 17.8 %slice-start = ((s8[12582912]{0:T(1024)(128)(4,1)}), s8[4194304]{0:T(1024)(128)(4,1)S(1)}, s32[]{:S(2)}) async-start(s8[12582912]{0:T(1024)(128)(4,1)} %bitcast.11), calls=%async_computation.1 | async-start | bytes 8388608
  115.1 2.2 %copy-start.1 = (bf16[144,12288]{1,0:T(8,128)(2,1)S(1)}, bf16[144,12288]{1,0:T(8,128)(2,1)}, u32[]{:S(2)}) copy-start(bf16[144,12288]{1,0:T(8,128)(2,1)} %copy-done) | copy-start | bytes 10616836
  117.2 2.2 %copy-start.3 = (bf16[144,12288]{1,0:T(8,128)(2,1)S(1)}, bf16[144,12288]{1,0:T(8,128)(2,1)}, u32[]{:S(2)}) copy-start(bf16[144,12288]{1,0:T(8,128)(2,1)} %copy-done.2) | copy-start | bytes 10616836
  119.4 13.4 %slice-start.1 = ((s8[12582912]{0:T(1024)(128)(4,1)}), s8[4194304]{0:T(1024)(128)(4,1)S(1)}, s32[]{:S(2)}) async-start(s8[12582912]{0:T(1024)(128)(4,1)} %bitcast.11), calls=%async_computation.2 | async-start | bytes 8388608
  119.4 13.4 %slice-start.2 = ((s8[12582912]{0:T(1024)(128)(4,1)}), s8[4194304]{0:T(1024)(128)(4,1)S(1)}, s32[]{:S(2)}) async-start(s8[12582912]{0:T(1024)(128)(4,1)} %bitcast.11), calls=%async_computation.3 | async-start | bytes 8388608
  140.8 2.4 %collective-permute-start.12 = (f32[384,512]{1,0:T(8,128)S(1)}, f32[384,512]{1,0:T(8,128)S(1)}, u32[]{:S(2)}, u32[]{:S(2)}) collective-permute-start(f32[384,512]{1,0:T(8,128)S(1)} %get-tuple-element.12), channel_id=1, source_target_pairs={{0,1},{1,0},{2,3},{3,2},{4,5},{5,4},{6,7},{7,6},{8,9},{9,8},{10,11... | collective-permute-start | bytes 2359304 | tf_op jit(solution)/shard_map/ppermute | solution.py:55
  143.4 12.4 %collective-permute-start.13 = (f32[96,512]{1,0:T(8,128)S(1)}, f32[96,512]{1,0:T(8,128)S(1)}, u32[]{:S(2)}, u32[]{:S(2)}) collective-permute-start(f32[96,512]{1,0:T(8,128)S(1)} %get-tuple-element.13), channel_id=1, source_target_pairs={{0,2},{1,3},{2,4},{3,5},{4,6},{5,7},{6,0},{7,1},{8,10},{9,11},{10,... | collective-permute-start | bytes 589832 | tf_op jit(solution)/shard_map/ppermute | solution.py:49
  144.0 11.8 %collective-permute-start.14 = (f32[96,512]{1,0:T(8,128)S(1)}, f32[96,512]{1,0:T(8,128)S(1)}, u32[]{:S(2)}, u32[]{:S(2)}) collective-permute-start(f32[96,512]{1,0:T(8,128)S(1)} %get-tuple-element.15), channel_id=1, source_target_pairs={{0,6},{1,7},{2,0},{3,1},{4,2},{5,3},{6,4},{7,5},{8,14},{9,15},{10,... | collective-permute-start | bytes 589832 | tf_op jit(solution)/shard_map/ppermute | solution.py:49
  146.7 9.1 %collective-permute-start.15 = (f32[96,512]{1,0:T(8,128)S(1)}, f32[96,512]{1,0:T(8,128)S(1)}, u32[]{:S(2)}, u32[]{:S(2)}) collective-permute-start(f32[96,512]{1,0:T(8,128)S(1)} %get-tuple-element.14), channel_id=1, source_target_pairs={{0,4},{1,5},{2,6},{3,7},{4,0},{5,1},{6,2},{7,3},{8,12},{9,13},{10,... | collective-permute-start | bytes 589832 | tf_op jit(solution)/shard_map/ppermute | solution.py:49
